TPU v7x, 32 devices: a whole 2x2x4 slice. The times are simulated.
32 devices in a mesh: ctx: 4 (over z), tp: 8 (over y, x, core).
Axes of the slice: x: 2, y: 2, z: 4, core: 2. Of those that a mesh axis runs over, the one named last changes fastest.
Arguments:
- q_nope: bfloat16 [512, 16384], P('ctx', 'tp'), may hold values from -5 to 5
- q_rope: bfloat16 [512, 8192], P('ctx', 'tp'), may hold values from -128 to 128
- cache_latent: bfloat16 [128, 576], P('ctx'), may hold values from -4 to 4
- group_latent: bfloat16 [512, 576], P('ctx'), may hold values from -4 to 4
- offset: int32 [1], replicated, may hold values from 128 to 255
- counts: int32 [4], replicated, may hold values from 1 to 32, as said below
- up_key: bfloat16 [128, 128, 512], P('tp'), may hold values from -0.5 to 0.5
- up_value: bfloat16 [128, 512, 128], P('tp'), may hold values from -0.25 to 0.25
- out_weight: bfloat16 [16384, 7168], P('tp'), may hold values from -0.0625 to 0.0625
Outputs:
- attn_out: bfloat16 [512, 7168], P('ctx', 'tp')
Inputs may be any that keep to these rules, and one draw needn't show every extreme that they name: counts[c] cache slots of context index c are live, the first ones; some index has all 32 live in every draw. `offset`: at least the number of cache slots in all.
All inputs are finite; a program needn't handle non-finite values.
Results may differ from a plain program's by a relative error of at most 0.025.
Values may be sent and summed in bfloat16 or wider, within the bound.
No kernel may reach another device: no remote copies, remote signals or barrier semaphores. Data moves between devices by JAX's collectives and lax.ppermute only.
A program may use at most 128 MiB of HBM per device.

v0:
```python
import math

import jax
import jax.numpy as jnp
from jax import lax
from jax.sharding import PartitionSpec as P

LATENT = 512
ROPE = 64
NOPE = 128
VDIM = 128


def rotate(values, positions):
    half_width = values.shape[-1] // 2
    frequency = 10000.0 ** (-2.0 * jnp.arange(half_width, dtype=jnp.float32) / ROPE)
    angles = positions.astype(jnp.float32)[:, None] * frequency[None, :]
    cosine = jnp.cos(angles)
    sine_part = jnp.sin(angles)
    if values.ndim == 3:
        cosine = cosine[:, None, :]
        sine_part = sine_part[:, None, :]
    front_half = values[..., :half_width].astype(jnp.float32)
    back_half = values[..., half_width:].astype(jnp.float32)
    joined = jnp.concatenate(
        [front_half * cosine - back_half * sine_part, back_half * cosine + front_half * sine_part],
        -1,
    )
    return joined.astype(jnp.bfloat16)


def local(q_nope, q_rope, cache_latent, group_latent, offset, counts, up_key, up_value, out_weight):
    tokens = q_nope.shape[0]
    head_count = up_key.shape[0]
    cached = cache_latent.shape[0]
    span_rows = cached + tokens
    position_base = lax.axis_index("ctx") * tokens
    positions = offset[0] + position_base + jnp.arange(tokens, dtype=jnp.int32)
    query_rope = rotate(q_rope.reshape(tokens, head_count, ROPE), positions)
    key_rope = rotate(group_latent[:, LATENT:], positions)
    group_keys = jnp.concatenate([group_latent[:, :LATENT], key_rope], 1)
    local_keys = jnp.concatenate([cache_latent, group_keys], 0)
    query_latent = jnp.einsum(
        "thn,hnl->thl",
        q_nope.reshape(tokens, head_count, NOPE),
        up_key,
        preferred_element_type=jnp.float32,
    ).astype(jnp.bfloat16)
    queries = jnp.concatenate([query_latent, query_rope], 2).reshape(
        tokens * head_count, LATENT + ROPE
    )
    query_token = position_base + jnp.arange(tokens * head_count, dtype=jnp.int32) // head_count
    owners = jnp.arange(counts.shape[0], dtype=jnp.int32)
    score_scale = 1.0 / math.sqrt(NOPE + ROPE)
    query_rows = tokens * head_count
    initial = (
        jnp.full((query_rows,), -1e30, jnp.float32),
        jnp.zeros((query_rows,), jnp.float32),
        jnp.zeros((query_rows, LATENT), jnp.float32),
    )
    key_block = lax.all_gather(local_keys, "ctx", axis=0, tiled=True)
    key_index = jnp.arange(key_block.shape[0], dtype=jnp.int32)
    key_owner = key_index // span_rows
    key_slot = key_index % span_rows
    live_count = jnp.sum(
        jnp.where(key_owner[:, None] == owners[None, :], counts[None, :], 0), axis=1
    )
    is_live = (key_slot < cached) & (key_slot < live_count)
    group_index = key_owner * tokens + key_slot - cached
    visible = is_live[None, :] | (key_slot >= cached)[None, :] & (
        group_index[None, :] <= query_token[:, None]
    )

    def update(current):
        row_max, row_sum, mixed_sum = current
        scores = (
            jnp.einsum("qd,kd->qk", queries, key_block, preferred_element_type=jnp.float32)
            * score_scale
        )
        scores = jnp.where(visible, scores, -jnp.inf)
        new_max = jnp.maximum(row_max, jnp.max(scores, axis=1))
        expos = jnp.exp(scores - new_max[:, None])
        row_sum = jnp.sum(expos, axis=1)
        mixed_sum = jnp.dot(
            expos.astype(jnp.bfloat16), key_block[:, :LATENT], preferred_element_type=jnp.float32
        )
        return (new_max, row_sum, mixed_sum)

    def unchanged(current):
        return current

    folded = lax.cond(jnp.any(visible), update, unchanged, initial)
    row_max, row_sum, mixed_sum = folded
    attended = (
        (mixed_sum / row_sum[:, None]).astype(jnp.bfloat16).reshape(tokens, head_count, LATENT)
    )
    head_out = jnp.einsum(
        "thl,hlv->thv", attended, up_value, preferred_element_type=jnp.float32
    ).astype(jnp.bfloat16)
    head_out = head_out.reshape(tokens, head_count * VDIM)
    summed = lax.psum_scatter(
        lax.dot_general(
            out_weight, head_out, (((0,), (1,)), ((), ())), preferred_element_type=jnp.float32
        ).astype(jnp.bfloat16),
        "tp",
        scatter_dimension=0,
        tiled=True,
    ).astype(jnp.float32)
    return summed.T.astype(jnp.bfloat16)


def solution(mesh):
    return jax.shard_map(
        local,
        mesh=mesh,
        in_specs=(
            P("ctx", "tp"),
            P("ctx", "tp"),
            P("ctx", None),
            P("ctx", None),
            P(),
            P(),
            P("tp", None, None),
            P("tp", None, None),
            P("tp", None),
        ),
        out_specs=P("ctx", "tp"),
        check_vma=False,
    )
```

profile of v0, /device:TPU:0, one launch (start us, length us, event | category | flops | bytes accessed | tf_op | source)
XLA Modules:
  0.0 127.8 jit_solution(11396052821741464700)
XLA Ops:
  6.5 0.0 copy-start
  6.5 0.0 reduce-scatter.4.cloned.1.call-start
  7.4 0.7 select_reduce_fusion
  8.2 0.9 slice.23
  9.1 0.9 fusion.19
  9.9 0.1 copy.47
  10.1 0.1 copy.48
  10.2 0.1 copy.56
  10.3 1.8 %copy.45 = bf16[128,1024]{0,1:T(8,128)(2,1)} copy(bf16[128,1024]{1,0:T(8,128)(2,1)} %param.12) | data formatting | bytes 524288 | tf_op args[1]
  12.1 0.9 maximum_maximum_fusion
  13.0 22.1 %all_gather.3 = bf16[640,576]{1,0:T(8,128)(2,1)} all-gather(bf16[160,576]{1,0:T(8,128)(2,1)S(1)} %maximum_maximum_fusion), channel_id=1, replica_groups=mesh['ctx'=4,'tp'=8] {'ctx'}, dimensions={0}, use_global_device_ids=true | all-gather | bytes 921600 | tf_op jit(solution)/shard_map/all_gather | solution.py:61
  35.1 2.2 %fusion.35 = (pred[]{:T(512)}, pred[2048,640]{0,1:T(32,128)(4,1)S(1)}) fusion(s32[2048]{0:T(1024)S(1)} %fusion.22, s32[640]{0:T(1024)S(1)} %add_add_fusion, pred[640]{0:T(1024)(128)(4,1)S(1)} %get-tuple-element.41, pred[640]{0:T(1024)(128)(4,1)S(1)} %get-tuple-element.42), kind=kLoop, calls=%fused_computation.65 | loop fusion | flops 5242879 | bytes 1322753 | tf_op jit(solution)/shard_map/reduce_or | solution.py:92
  37.9 0.0 copy-done
  37.9 0.0 copy-start.1
  38.0 1.9 %convert_bitcast_fusion = bf16[128,16,512]{0,2,1:T(8,128)(2,1)S(1)} fusion(bf16[16,128,512]{2,1,0:T(8,128)(2,1)S(1)} %copy-done, bf16[128,2048]{1,0:T(8,128)(2,1)} %param.11), kind=kOutput, calls=%fused_computation.15 | convolution fusion | flops 269484032 | bytes 4718592 | tf_op jit(solution)/shard_map/thn,hnl->thl/dot_general | solution.py:43
  39.8 0.0 copy-done.1
  39.8 0.1 fusion.15
  39.9 1.6 %pad_maximum_fusion = bf16[128,16,576]{0,2,1:T(8,128)(2,1)} fusion(bf16[128,16,32]{0,2,1:T(8,128)(2,1)S(1)} %get-tuple-element.36, bf16[128,16,32]{0,2,1:T(8,128)(2,1)S(1)} %get-tuple-element.35, bf16[128,16,512]{0,2,1:T(8,128)(2,1)S(1)} %convert_bitcast_fusion), kind=kLoop, calls=%fused_computation.12 | loop fusion | flops 7077888 | bytes 4718592 | tf_op jit(solution)/shard_map/concatenate | solution.py:49
  41.5 14.2 %conditional.1 = (f32[2048]{0:T(1024)S(1)}, f32[2048,512]{1,0:T(8,128)}) conditional(s32[]{:T(128)} %convert_element_type.54, () %tuple.13, (bf16[128,16,576]{0,2,1:T(8,128)(2,1)}, bf16[640,576]{1,0:T(8,128)(2,1)}, pred[2048,640]{0,1:T(32,128)(4,1)S(1)}) %tuple.14), branch_computations={%region_2.3_spmd, %region_3.6_spmd} | conditional | flops 2861299712 | bytes 32702508 | solution.py:92
  41.5 4.9 %copy.49 = bf16[128,16,576]{2,1,0:T(8,128)(2,1)} copy(bf16[128,16,576]{0,2,1:T(8,128)(2,1)} %get-tuple-element.28) | data formatting | bytes 4718592 | tf_op jit(solution)/shard_map
  46.4 4.3 %fusion.36 = (f32[2048]{0:T(1024)S(1)}, f32[2048,640]{0,1:T(8,128)S(1)}) fusion(pred[2048,640]{0,1:T(32,128)(4,1)S(1)} %get-tuple-element.12, bf16[2048,576]{1,0:T(8,128)(2,1)} %bitcast.27, bf16[640,576]{1,0:T(8,128)(2,1)} %get-tuple-element.14), kind=kOutput, calls=%fused_computation.66 | convolution fusion | flops 1513879552 | bytes 9658368 | tf_op jit(solution)/shard_map/cond/branch_1_fun/qd,kd->qk/dot_general | solution.py:77
  50.8 0.0 copy-start.2
  50.8 0.7 fusion.1
  51.5 0.4 copy-done.2
  51.9 3.8 %fusion.2 = f32[2048,512]{1,0:T(8,128)} fusion(f32[2048,640]{0,1:T(8,128)S(1)} %get-tuple-element.34, f32[2048]{0:T(1024)S(1)} %broadcast_maximum_fusion, bf16[640,576]{1,0:T(8,128)(2,1)S(1)} %copy-done.2), kind=kOutput, calls=%fused_computation.4 | convolution fusion | flops 1344798720 | bytes 10100736 | tf_op jit(solution)/shard_map/cond/branch_1_fun/dot_general | solution.py:84
  55.7 0.0 copy-start.3
  55.7 2.7 %divide_convert_fusion = bf16[2048,512]{1,0:T(8,128)(2,1)S(1)} fusion(f32[2048,512]{1,0:T(8,128)} %get-tuple-element.17, f32[2048]{0:T(1024)S(1)} %get-tuple-element.18), kind=kLoop, calls=%fused_computation.11 | loop fusion | flops 2097152 | bytes 6299648 | tf_op jit(solution)/shard_map/convert_element_type | solution.py:95
  58.4 0.1 copy-done.3
  58.5 2.7 %fusion.9 = bf16[16,128,128]{1,2,0:T(8,128)(2,1)S(1)} fusion(bf16[16,512,128]{2,1,0:T(8,128)(2,1)S(1)} %copy-done.3, bf16[128,16,512]{2,1,0:T(8,128)(2,1)S(1)} %bitcast.28), kind=kOutput, calls=%fused_computation.16 | convolution fusion | flops 268697600 | bytes 4718592 | tf_op jit(solution)/shard_map/thl,hlv->thv/dot_general | solution.py:97
  61.2 14.8 %fusion.6 = bf16[7168,128]{0,1:T(8,128)(2,1)} fusion(bf16[128,2048]{0,1:T(8,128)(2,1)S(1)} %bitcast.30, bf16[2048,7168]{1,0:T(8,128)(2,1)} %param.19), kind=kOutput, calls=%fused_computation.9 | convolution fusion | flops 3759013888 | bytes 31719424 | tf_op jit(solution)/shard_map/dot_general | solution.py:102
  76.0 3.9 %copy.54 = bf16[7168,128]{1,0:T(8,128)(2,1)} copy(bf16[7168,128]{0,1:T(8,128)(2,1)} %fusion.6) | data formatting | bytes 3670016
  79.9 0.0 reduce-scatter.4.cloned.1.call-update
  79.9 39.2 %reduce-scatter.4.cloned.1.call-done = bf16[896,128]{1,0:T(8,128)(2,1)} async-done(((bf16[7168,128]{1,0:T(8,128)(2,1)}), bf16[896,128]{1,0:T(8,128)(2,1)}) %reduce-scatter.4.cloned.1.call-update) | async-done | bytes 229392
  119.2 1.8 %copy.55 = bf16[896,128]{0,1:T(8,128)(2,1)} copy(bf16[896,128]{1,0:T(8,128)(2,1)} %reduce-scatter.4.cloned.1.call-done) | data formatting | bytes 458752
  (7 shorter events, 0.1 us)
Async XLA Ops:
  6.5 31.4 %copy-start = (bf16[16,128,512]{2,1,0:T(8,128)(2,1)S(1)}, bf16[16,128,512]{2,1,0:T(8,128)(2,1)}, u32[]{:S(2)}) copy-start(bf16[16,128,512]{2,1,0:T(8,128)(2,1)} %param.17) | copy-start | bytes 6291460
  6.5 112.6 %reduce-scatter.4.cloned.1.call-start = ((), (), s32[]{:S(2)}) async-start(), calls=%async_computation.1 | async-start | bytes 2064384
  37.9 1.9 %copy-start.1 = (bf16[128,1024]{0,1:T(8,128)(2,1)S(1)}, bf16[128,1024]{0,1:T(8,128)(2,1)}, u32[]{:S(2)}) copy-start(bf16[128,1024]{0,1:T(8,128)(2,1)} %copy.45) | copy-start | bytes 786436
  50.8 1.1 copy-start.2
  55.7 2.9 %copy-start.3 = (bf16[16,512,128]{2,1,0:T(8,128)(2,1)S(1)}, bf16[16,512,128]{2,1,0:T(8,128)(2,1)}, u32[]{:S(2)}) copy-start(bf16[16,512,128]{2,1,0:T(8,128)(2,1)} %param.18) | copy-start | bytes 6291460
Sparse Core Ops, SparseCore 0:
  80.0 39.0 reduce-scatter.3
where the time goes:
time: 128 us
  waiting for transfers between devices  39.3 us (31%)
  matrix products  27.4 us (21%)
  blocking collectives  22.1 us (17%)
  between operations  14.9 us (12%)
  local copies, waits for them, and re-layouts  14.2 us (11%)
  other arithmetic  9.85 us (8%)
    unnamed x2, waiting for transfers between devices  39.3 us
    all_gather x1, blocking collectives, local(): key_block = lax.all_gather(local_keys, 'ctx', axis=0, tiled=True)  22.1 us
    dot_general x1, matrix products, local(): lax.dot_general(out_weight, head_out, (((0,), (1,)), ((), ())), preferred...  14.8 us
    unnamed x10, local copies, waits for them, and re-layouts  7.73 us
    another operation x3, local copies, waits for them, and re-layouts  5.15 us
    dot_general x1, matrix products, update(): jnp.einsum('qd,kd->qk', queries, key_block, preferred_element_type=jnp.fl...  4.32 us
    dot_general x1, matrix products, update(): jnp.dot(expos.astype(jnp.bfloat16), key_block[:, :LATENT], preferred_elem...  3.78 us
    convert_element_type x1, other arithmetic, local(): (mixed_sum / row_sum[:, None]).astype(jnp.bfloat16)  2.7 us
  transfers between devices with their start and end apart: 1, of which 1 were waited for; matrix products, arithmetic and copies ran while one was open for 0% of the time, Pallas kernels for 0%

commit v1 on v0

v1 whole, which is shorter than its diff:
```python
import functools
import math

import jax
import jax.numpy as jnp
from jax import lax
from jax.experimental import pallas as pl
from jax.experimental.pallas import tpu as pltpu
from jax.sharding import PartitionSpec as P

LATENT = 512
ROPE = 64
NOPE = 128
VDIM = 128
LANES = 128
HIDDEN = -1e30
LOG2E = 1.4426950408889634


def widen(width):
    return -(-width // LANES) * LANES


def rope_tables(positions, live):
    half = ROPE // 2
    frequency = 10000.0 ** (-2.0 * jnp.arange(half, dtype=jnp.float32) / ROPE)
    angles = positions.astype(jnp.float32)[:, None] * frequency[None, :]
    cosine = jnp.where(live[:, None], jnp.cos(angles), 1.0)
    sine = jnp.where(live[:, None], jnp.sin(angles), 0.0)
    return jnp.concatenate([cosine, cosine], 1), jnp.concatenate([-sine, sine], 1)


def query_kernel(nope_ref, rope_ref, up_ref, cos_ref, sin_ref, out_ref):
    heads = up_ref.shape[0]
    pad = out_ref.shape[2] - LATENT - ROPE
    half = ROPE // 2
    for head in range(heads):
        nope = nope_ref[:, head * NOPE : (head + 1) * NOPE]
        latent = jnp.dot(nope, up_ref[head], preferred_element_type=jnp.float32)
        out_ref[head, :, :LATENT] = latent.astype(jnp.bfloat16)
        raw = rope_ref[:, head * ROPE : (head + 1) * ROPE].astype(jnp.float32)
        swapped = jnp.concatenate([raw[:, half:], raw[:, :half]], 1)
        turned = raw * cos_ref[...] + swapped * sin_ref[...]
        filled = jnp.concatenate([turned, jnp.zeros((raw.shape[0], pad), jnp.float32)], 1)
        out_ref[head, :, LATENT:] = filled.astype(jnp.bfloat16)


def make_queries(q_nope, q_rope, up_key, cosine, sine):
    tokens = q_nope.shape[0]
    heads = up_key.shape[0]
    pair = LANES // ROPE
    width = widen(LATENT + ROPE)
    return pl.pallas_call(
        query_kernel,
        grid=(heads // pair,),
        in_specs=[
            pl.BlockSpec((tokens, pair * NOPE), lambda g: (0, g)),
            pl.BlockSpec((tokens, pair * ROPE), lambda g: (0, g)),
            pl.BlockSpec((pair, NOPE, LATENT), lambda g: (g, 0, 0)),
            pl.BlockSpec((tokens, ROPE), lambda g: (0, 0)),
            pl.BlockSpec((tokens, ROPE), lambda g: (0, 0)),
        ],
        out_specs=pl.BlockSpec((pair, tokens, width), lambda g: (g, 0, 0)),
        out_shape=jax.ShapeDtypeStruct((heads, tokens, width), jnp.bfloat16),
        name="queries",
        cost_estimate=pl.CostEstimate(
            flops=2 * heads * tokens * NOPE * LATENT, bytes_accessed=6 << 20, transcendentals=0
        ),
    )(q_nope, q_rope, up_key, cosine, sine)


def attend_kernel(
    q_ref, mine_ref, theirs_ref, cache_ref, group_ref, from_ref, cos_ref, sin_ref, row_ref, up_ref,
    out_ref, keys_ref,
):
    half = ROPE // 2
    shifts = mine_ref.shape[0]
    part_rows = mine_ref.shape[1]

    @pl.when(pl.program_id(0) == 0)
    def _():
        def put(raw, start):
            rows = raw.shape[0]
            keys_ref[start : start + rows, :LATENT] = raw[:, :LATENT]
            tail = raw[:, LATENT:].astype(jnp.float32)
            swapped = jnp.concatenate([tail[:, half:], tail[:, :half]], 1)
            turned = tail * cos_ref[start : start + rows] + swapped * sin_ref[start : start + rows]
            pad = keys_ref.shape[1] - LATENT - ROPE
            filled = jnp.concatenate([turned, jnp.zeros((rows, pad), jnp.float32)], 1)
            keys_ref[start : start + rows, LATENT:] = filled.astype(jnp.bfloat16)

        for shift in range(shifts):
            put(mine_ref[shift], 2 * shift * part_rows)
            put(theirs_ref[shift], (2 * shift + 1) * part_rows)
        base = 2 * shifts * part_rows
        put(cache_ref[...], base)
        put(group_ref[...], base + cache_ref.shape[0])

    heads, tokens, width = q_ref.shape
    queries = q_ref[...].reshape(heads * tokens, width)
    scores = lax.dot_general(
        queries, keys_ref[...], (((1,), (1,)), ((), ())), preferred_element_type=jnp.float32
    )
    scale = LOG2E / math.sqrt(NOPE + ROPE)
    visible = from_ref[...] <= row_ref[...]
    bias = jnp.where(visible, 0.0, HIDDEN)
    scores = scores.reshape(heads, tokens, -1) + bias[None]
    peak = jnp.max(scores, axis=2, keepdims=True)
    expos = jnp.exp2((scores - peak) * scale)
    total = jnp.sum(expos, axis=2, keepdims=True)
    weights = expos.astype(jnp.bfloat16).reshape(heads * tokens, -1)
    mixed = jnp.dot(weights, keys_ref[:, :LATENT], preferred_element_type=jnp.float32)
    attended = (mixed.reshape(heads, tokens, LATENT) / total).astype(jnp.bfloat16)
    for head in range(heads):
        value = jnp.dot(attended[head], up_ref[head], preferred_element_type=jnp.float32)
        out_ref[:, head * VDIM : (head + 1) * VDIM] = value.astype(jnp.bfloat16)


def attend(queries, mine, theirs, cache, group, visible_from, cosine, sine, rows, up_value):
    heads, tokens, width = queries.shape
    total = visible_from.shape[1]
    step = heads
    while step > 1 and step * tokens * total * 4 > (3 << 20) // 2:
        step //= 2
    whole = lambda a: pl.BlockSpec(a.shape, lambda g: (0,) * a.ndim)
    return pl.pallas_call(
        attend_kernel,
        grid=(heads // step,),
        in_specs=[
            pl.BlockSpec((step, tokens, width), lambda g: (g, 0, 0)),
            whole(mine),
            whole(theirs),
            whole(cache),
            whole(group),
            whole(visible_from),
            whole(cosine),
            whole(sine),
            whole(rows),
            pl.BlockSpec((step, LATENT, VDIM), lambda g: (g, 0, 0)),
        ],
        out_specs=pl.BlockSpec((tokens, step * VDIM), lambda g: (0, g)),
        out_shape=jax.ShapeDtypeStruct((tokens, heads * VDIM), jnp.bfloat16),
        scratch_shapes=[pltpu.VMEM((total, width), jnp.bfloat16)],
        name="attend",
        cost_estimate=pl.CostEstimate(
            flops=2 * heads * tokens * total * (LATENT + width),
            bytes_accessed=8 << 20,
            transcendentals=heads * tokens * total,
        ),
    )(queries, mine, theirs, cache, group, visible_from, cosine, sine, rows, up_value)


def project_kernel(order_ref, head_ref, weight_ref, out_ref):
    out_ref[0] = jnp.dot(
        head_ref[...], weight_ref[...], preferred_element_type=jnp.float32
    ).astype(jnp.bfloat16)


def project(order, head_out, weight, width):
    tokens, depth = head_out.shape
    blocks = order.shape[0]
    return pl.pallas_call(
        project_kernel,
        grid_spec=pltpu.PrefetchScalarGridSpec(
            num_scalar_prefetch=1,
            grid=(blocks,),
            in_specs=[
                pl.BlockSpec((tokens, depth), lambda i, order: (0, 0)),
                pl.BlockSpec((depth, width), lambda i, order: (0, order[i])),
            ],
            out_specs=pl.BlockSpec((1, tokens, width), lambda i, order: (i, 0, 0)),
        ),
        out_shape=jax.ShapeDtypeStruct((blocks, tokens, width), jnp.bfloat16),
        name="project",
        cost_estimate=pl.CostEstimate(
            flops=2 * blocks * tokens * depth * width,
            bytes_accessed=2 * blocks * depth * width,
            transcendentals=0,
        ),
    )(order, head_out, weight)


def local(ctx_size, tp_size, q_nope, q_rope, cache_latent, group_latent, offset, counts, up_key, up_value, out_weight):
    tokens = q_nope.shape[0]
    cached = cache_latent.shape[0]
    ctx = lax.axis_index("ctx")
    tp = lax.axis_index("tp")
    core = tp % 2
    swap = [(i, i ^ 1) for i in range(tp_size)]

    part = jnp.concatenate(
        [
            lax.dynamic_slice_in_dim(cache_latent, core * (cached // 2), cached // 2, 0),
            lax.dynamic_slice_in_dim(group_latent, core * (tokens // 2), tokens // 2, 0),
        ],
        0,
    )
    arrived = [
        lax.ppermute(part, "ctx", [(i, (i + shift) % ctx_size) for i in range(ctx_size)])
        for shift in range(1, ctx_size)
    ]
    mine = jnp.stack(arrived)
    theirs = lax.ppermute(mine, "tp", swap)

    part_rows = part.shape[0]
    slot = jnp.arange(part_rows, dtype=jnp.int32)
    owner = (ctx - jnp.arange(1, ctx_size, dtype=jnp.int32) + ctx_size) % ctx_size
    side = jnp.stack([core, 1 - core]).astype(jnp.int32)
    in_cache = slot < cached // 2
    cache_slot = side[:, None] * (cached // 2) + slot[None]
    group_slot = side[:, None] * (tokens // 2) + slot[None] - cached // 2
    far = jnp.int32(1 << 30)

    def marks(owners, cache_slots, group_slots, cache_mask):
        live = jnp.where(cache_slots < counts[owners], -1, far)
        position = owners * tokens + group_slots
        return jnp.where(cache_mask, live, position), position, ~cache_mask

    shape = (ctx_size - 1, 2, part_rows)
    remote = marks(
        jnp.broadcast_to(owner[:, None, None], shape),
        jnp.broadcast_to(cache_slot[None], shape),
        jnp.broadcast_to(group_slot[None], shape),
        jnp.broadcast_to(in_cache[None, None], shape),
    )
    own_slot = jnp.arange(cached + tokens, dtype=jnp.int32)
    own = marks(jnp.full_like(own_slot, ctx), own_slot, own_slot - cached, own_slot < cached)
    visible_from, position, rotated = (
        jnp.concatenate([a.reshape(-1), b]) for a, b in zip(remote, own)
    )
    key_cos, key_sin = rope_tables(offset[0] + position, rotated)
    rows = ctx * tokens + jnp.arange(tokens, dtype=jnp.int32)
    row_cos, row_sin = rope_tables(offset[0] + rows, jnp.ones((tokens,), bool))

    queries = make_queries(q_nope, q_rope, up_key, row_cos, row_sin)
    head_out = attend(
        queries, mine, theirs, cache_latent, group_latent, visible_from[None], key_cos, key_sin,
        rows[:, None], up_value,
    )

    features = out_weight.shape[1]
    width = features // tp_size
    chips = tp_size // 2
    if width % LANES or chips & (chips - 1):
        partial = jnp.dot(head_out, out_weight, preferred_element_type=jnp.float32)
        summed = lax.psum_scatter(
            partial.astype(jnp.bfloat16), "tp", scatter_dimension=1, tiled=True
        )
        return summed.astype(jnp.bfloat16)

    chip = tp // 2
    order = [delta for delta in range(chips - 1, -1, -1)]
    blocks = jnp.stack([2 * (chip ^ delta) for delta in order]).astype(jnp.int32)
    sent = project(blocks + (1 - core), head_out, out_weight, width)
    swapped = lax.ppermute(sent, "tp", swap)
    kept = project(blocks + core, head_out, out_weight, width)
    both = kept.astype(jnp.float32) + swapped.astype(jnp.float32)
    total = both[chips - 1]
    for place, delta in enumerate(order[:-1]):
        moved = lax.ppermute(
            both[place].astype(jnp.bfloat16), "tp", [(i, i ^ (2 * delta)) for i in range(tp_size)]
        )
        total = total + moved.astype(jnp.float32)
    return total.astype(jnp.bfloat16)


def solution(mesh):
    return jax.shard_map(
        functools.partial(local, mesh.shape["ctx"], mesh.shape["tp"]),
        mesh=mesh,
        in_specs=(
            P("ctx", "tp"),
            P("ctx", "tp"),
            P("ctx", None),
            P("ctx", None),
            P(),
            P(),
            P("tp", None, None),
            P("tp", None, None),
            P("tp", None),
        ),
        out_specs=P("ctx", "tp"),
        check_vma=False,
    )
```

time: 128 us -> 75.1 us (0.59)
  Pallas kernels: 0 us -> 33.6 us
  waiting for transfers between devices: 39.3 us -> 10 us
  matrix products: 27.4 us -> 0 us
  blocking collectives: 22.1 us -> 0 us
  between operations: 14.9 us -> 3.24 us
  starting transfers between devices: 0.01 us -> 10.2 us
  local copies, waits for them, and re-layouts: 14.2 us -> 8.59 us
    unnamed x2 -> x0, waiting for transfers between devices: 39.3 us -> none
    pallas_call x0 -> x4, Pallas kernels: none -> 33.6 us  [the longest x2 17.2 us: project(): pl.pallas_call(project_kernel, grid_spec=pltpu.PrefetchScalarGridSpec(num...]
    dot_general x5 -> x0, matrix products: 27.4 us -> none  [the longest x1 14.8 us: local(): lax.dot_general(out_weight, head_out, (((0,), (1,)), ((), ())), preferred...]
    all_gather x1 -> x0, blocking collectives: 22.1 us -> none  [local(): key_block = lax.all_gather(local_keys, 'ctx', axis=0, tiled=True)]
    ppermute x0 -> x8, starting transfers between devices: none -> 10.2 us  [the longest x3 6.14 us: local(): lax.ppermute(part, 'ctx', [(i, (i + shift) % ctx_size) for i in range(ctx...]
    ppermute x0 -> x8, waiting for transfers between devices: none -> 10 us  [the longest x3 10 us: local(): lax.ppermute(both[place].astype(jnp.bfloat16), 'tp', [(i, i ^ 2 * delta)...]
    unnamed x10 -> x9, local copies, waits for them, and re-layouts: 7.73 us -> 1.8 us
    another operation x3 -> x0, local copies, waits for them, and re-layouts: 5.15 us -> none
  transfers between devices with their start and end apart: 1 -> 8, of which waited for: 1 -> 3; matrix products, arithmetic and copies ran while one was open for 0% -> 17% of each run, Pallas kernels for 0% -> 21%
where the time goes in v1:
time: 75.1 us; the launch traced here: 74.6 us
  Pallas kernels  33.6 us (45%)
  starting transfers between devices  10.2 us (14%)
  waiting for transfers between devices  10 us (13%)
  other arithmetic  8.93 us (12%)
  local copies, waits for them, and re-layouts  8.59 us (11%)
  between operations  3.24 us (4%)
    pallas_call x2, Pallas kernels, project(): pl.pallas_call(project_kernel, grid_spec=pltpu.PrefetchScalarGridSpec(num...  17.2 us
    ppermute x3, waiting for transfers between devices, local(): lax.ppermute(both[place].astype(jnp.bfloat16), 'tp', [(i, i ^ 2 * delta)...  10 us
    pallas_call x1, Pallas kernels, attend(): pl.pallas_call(attend_kernel, grid=(heads // step,), in_specs=[pl.BlockSp...  9.55 us
    pallas_call x1, Pallas kernels, make_queries(): pl.pallas_call(query_kernel, grid=(heads // pair,), in_specs=[pl.BlockSpe...  6.87 us
    ppermute x3, starting transfers between devices, local(): lax.ppermute(part, 'ctx', [(i, (i + shift) % ctx_size) for i in range(ctx...  6.14 us
    gather x3, local copies, waits for them, and re-layouts, marks(): live = jnp.where(cache_slots < counts[owners], -1, far)  4.89 us
    ppermute x3, starting transfers between devices, local(): lax.ppermute(both[place].astype(jnp.bfloat16), 'tp', [(i, i ^ 2 * delta)...  3.55 us
    unnamed x9, local copies, waits for them, and re-layouts  1.8 us
  transfers between devices with their start and end apart: 8, of which 3 were waited for; matrix products, arithmetic and copies ran while one was open for 17% of the time, Pallas kernels for 21%

profile of v1, /device:TPU:0, one launch (start us, length us, event | category | flops | bytes accessed | tf_op | source)
XLA Modules:
  0.0 74.6 jit_solution(18374286368751430457)
XLA Ops:
  0.0 1.1 %copy.15.group_ref = bf16[128,576]{1,0:T(8,128)(2,1)S(1)} copy(bf16[128,576]{0,1:T(8,128)(2,1)} %param.12) | data formatting | bytes 294912 | tf_op args[3]
  1.1 0.0 copy-start.1
  1.1 0.8 %constant_dynamic-slice_fusion.1 = bf16[16,576]{1,0:T(8,128)(2,1)S(1)} fusion(bf16[32,576]{1,0:T(8,128)(2,1)} %cache_ref.1, s32[]{:T(128)S(6)} %select_n.74), kind=kLoop, calls=%fused_computation.50 | loop fusion | bytes 36868 | tf_op jit(solution)/shard_map/dynamic_slice | solution.py:193
  1.9 5.1 %collective-permute-start.2 = (bf16[80,576]{1,0:T(8,128)(2,1)S(1)}, bf16[80,576]{1,0:T(8,128)(2,1)S(1)}, u32[]{:S(2)}, u32[]{:S(2)}) collective-permute-start(bf16[80,576]{1,0:T(8,128)(2,1)S(1)} %pad_maximum_fusion.3), channel_id=1, source_target_pairs={{0,24},{8,0},{16,8},{24,16},{1,25},{9,1},{17,9},{25,17},{2,26},{10... | collective-permute-start | bytes 276488 | tf_op jit(solution)/shard_map/ppermute | solution.py:199
  7.0 0.0 collective-permute-start.1
  7.0 1.0 %collective-permute-start = (bf16[80,576]{1,0:T(8,128)(2,1)S(1)}, bf16[80,576]{1,0:T(8,128)(2,1)S(1)}, u32[]{:S(2)}, u32[]{:S(2)}) collective-permute-start(bf16[80,576]{1,0:T(8,128)(2,1)S(1)} %pad_maximum_fusion.3), channel_id=1, source_target_pairs={{0,8},{8,16},{16,24},{24,0},{1,9},{9,17},{17,25},{25,1},{2,10},{10... | collective-permute-start | bytes 276488 | tf_op jit(solution)/shard_map/ppermute | solution.py:199
  8.8 0.6 iota_add_fusion.row_ref
  9.5 0.1 broadcast_in_dim.102
  9.5 0.1 reshape.153
  9.6 0.1 broadcast_multiply_fusion
  9.7 0.1 add_add_fusion.2
  9.8 0.1 iota_add_fusion.1
  9.9 0.1 broadcast_add_fusion
  9.9 0.1 add.186
  10.0 0.1 broadcast_select_fusion
  10.1 0.1 reshape.156
  10.2 1.5 %fusion.14 = (s32[1]{0:T(128)}, s32[1]{0:T(128)}, s32[1]{0:T(128)}, s32[1]{0:T(128)}) fusion(s32[4]{0:T(128)} %param.14), kind=kLoop, calls=%fused_computation.60 | loop fusion | bytes 32 | tf_op jit(solution)/shard_map/gather | solution.py:215
  11.7 3.3 %gather_fusion = s32[480]{0:T(512)S(1)} fusion(s32[4]{0:T(128)S(1)} %copy-done, s32[1024]{0:T(1024)S(1)} %pad_clamp_fusion), kind=kCustom, calls=%fused_computation | custom fusion | bytes 5760 | tf_op jit(solution)/shard_map/gather | solution.py:215
  15.0 0.1 reshape.155
  15.1 0.1 select_n.79
  17.6 0.1 pad_add_fusion.1
  17.7 0.3 fusion.7
  18.0 0.1 fusion.8
  18.1 1.3 %fusion.6 = (f32[640,32]{1,0:T(8,128)S(1)}, f32[640,32]{1,0:T(8,128)S(1)}, f32[640,32]{1,0:T(8,128)S(1)}) fusion(f32[32]{0:T(128)S(1)} %multiply_power_fusion, f32[640]{0:T(1024)S(1)} %fusion.8, pred[640]{0:T(1024)(128)(4,1)S(1)} %pad_add_fusion.1), kind=kLoop, calls=%fused_computation.20 | loop fusion | flops 81920 | bytes 249088 | tf_op jit(solution)/shard_map/neg | solution.py:30
  19.4 0.9 %pad_maximum_fusion.cos_ref = f32[640,64]{1,0:T(8,128)} fusion(f32[640,32]{1,0:T(8,128)S(1)} %get-tuple-element.14), kind=kLoop, calls=%fused_computation.11 | loop fusion | flops 40960 | bytes 245760 | tf_op jit(solution)/shard_map/concatenate | solution.py:30
  20.3 0.9 %pad_maximum_fusion.1.sin_ref = f32[640,64]{1,0:T(8,128)} fusion(f32[640,32]{1,0:T(8,128)S(1)} %get-tuple-element.13, f32[640,32]{1,0:T(8,128)S(1)} %get-tuple-element.12), kind=kLoop, calls=%fused_computation.12 | loop fusion | flops 40960 | bytes 327680 | tf_op jit(solution)/shard_map/concatenate | solution.py:30
  21.2 0.8 %pad_maximum_fusion.4 = (f32[128,64]{1,0:T(8,128)}, f32[128,64]{1,0:T(8,128)}) fusion(f32[128,32]{1,0:T(8,128)S(1)} %get-tuple-element.17, f32[128,32]{1,0:T(8,128)S(1)} %get-tuple-element.16, f32[128,32]{1,0:T(8,128)S(1)} %get-tuple-element.15), kind=kLoop, calls=%fused_computation.21 | loop fusion | flops 16384 | bytes 114688 | tf_op jit(solution)/shard_map/concatenate | solution.py:30
  21.9 0.1 pad_add_fusion
  22.0 0.1 pad_maximum_fusion.2.mine_ref
  22.1 0.1 collective-permute-start.3
  22.2 0.7 broadcast_add_fusion.3
  22.8 0.6 broadcast_in_dim.115.from_ref
  23.4 6.9 %queries.1.q_ref = bf16[16,128,640]{2,1,0:T(8,128)(2,1)} custom-call(bf16[128,2048]{1,0:T(8,128)(2,1)} %nope_ref.1, bf16[128,1024]{1,0:T(8,128)(2,1)} %rope_ref.1, bf16[16,128,512]{2,1,0:T(8,128)(2,1)} %up_ref.2, f32[128,64]{1,0:T(8,128)} %get-tuple-element.26.cos_ref, f32[128,64]{1,0:T(8,128)} %get-tuple-element.27.sin_ref), custom_call_target="tpu_custom_call" | custom-call | flops 268435456 | bytes 6291456 | tf_op jit(solution)/shard_map/queries/pallas_call | solution.py:53
  30.3 0.5 broadcast_add_fusion.1.order_ref
  30.8 0.7 copy-done.3
  31.5 9.5 %attend.1.head_ref = bf16[128,2048]{1,0:T(8,128)(2,1)} custom-call(bf16[16,128,640]{2,1,0:T(8,128)(2,1)} %queries.1.q_ref, bf16[3,80,576]{2,1,0:T(8,128)(2,1)} %copy-done.2, bf16[3,80,576]{2,1,0:T(8,128)(2,1)} %copy-done.3, bf16[32,576]{1,0:T(8,128)(2,1)} %cache_ref.1, bf16[128,576]{1,0:T(8,128)(2,1)} %copy-done.1, s32[1,640]{1,0:T(1,128)} %broadcast_in_dim.115.from_ref, ...), custom_call_target="tpu_custom_call" | custom-call | flops 3019898880 | bytes 8388608 | tf_op jit(solution)/shard_map/attend/pallas_call | solution.py:126
  41.1 8.6 %project.3 = bf16[4,128,896]{2,1,0:T(8,128)(2,1)} custom-call(s32[4]{0:T(128)} %broadcast_add_fusion.1.order_ref, bf16[128,2048]{1,0:T(8,128)(2,1)} %attend.1.head_ref, bf16[2048,7168]{1,0:T(8,128)(2,1)} %weight_ref.3), custom_call_target="tpu_custom_call" | custom-call | flops 1879048192 | bytes 14680064 | tf_op jit(solution)/shard_map/project/pallas_call | solution.py:162
  49.7 0.4 collective-permute-start.4
  50.1 8.6 %project.2 = bf16[4,128,896]{2,1,0:T(8,128)(2,1)} custom-call(s32[4]{0:T(128)} %get-tuple-element.5.order_ref, bf16[128,2048]{1,0:T(8,128)(2,1)} %attend.1.head_ref, bf16[2048,7168]{1,0:T(8,128)(2,1)} %weight_ref.3), custom_call_target="tpu_custom_call" | custom-call | flops 1879048192 | bytes 14680064 | tf_op jit(solution)/shard_map/project/pallas_call | solution.py:162
  58.7 1.5 %fusion.13 = (bf16[4,128,896]{2,1,0:T(8,128)(2,1)S(1)}, f32[4,128,896]{2,1,0:T(8,128)S(1)}) fusion(bf16[4,128,896]{2,1,0:T(8,128)(2,1)S(1)} %collective-permute-done.4, bf16[4,128,896]{2,1,0:T(8,128)(2,1)} %project.2), kind=kLoop, calls=%fused_computation.59 | loop fusion | flops 1835008 | bytes 4587520 | tf_op jit(solution)/shard_map/convert.2
  60.1 0.1 slice_bitcast_fusion.3
  60.2 2.5 %collective-permute-start.5 = (bf16[128,896]{1,0:T(8,128)(2,1)S(1)}, bf16[128,896]{1,0:T(8,128)(2,1)S(1)}, u32[]{:S(2)}, u32[]{:S(2)}) collective-permute-start(bf16[128,896]{1,0:T(8,128)(2,1)S(1)} %get-tuple-element.9), channel_id=1, source_target_pairs={{0,6},{1,7},{2,4},{3,5},{4,2},{5,3},{6,0},{7,1},{8,14},{9,15},{10,... | collective-permute-start | bytes 688136 | tf_op jit(solution)/shard_map/ppermute | solution.py:260
  62.7 0.5 collective-permute-start.7
  63.2 0.6 collective-permute-start.6
  63.8 5.9 %collective-permute-done.5 = bf16[128,896]{1,0:T(8,128)(2,1)S(1)} collective-permute-done((bf16[128,896]{1,0:T(8,128)(2,1)S(1)}, bf16[128,896]{1,0:T(8,128)(2,1)S(1)}, u32[]{:S(2)}, u32[]{:S(2)}) %collective-permute-start.5) | collective-permute-done | bytes 229408 | tf_op jit(solution)/shard_map/ppermute | solution.py:260
  69.7 4.0 %collective-permute-done.7 = bf16[128,896]{1,0:T(8,128)(2,1)S(1)} collective-permute-done((bf16[128,896]{1,0:T(8,128)(2,1)S(1)}, bf16[128,896]{1,0:T(8,128)(2,1)S(1)}, u32[]{:S(2)}, u32[]{:S(2)}) %collective-permute-start.7) | collective-permute-done | bytes 229408 | tf_op jit(solution)/shard_map/ppermute | solution.py:260
  73.7 0.1 collective-permute-done.6
  73.8 0.8 %fusion.3 = bf16[128,896]{1,0:T(8,128)(2,1)} fusion(f32[4,128,896]{2,1,0:T(8,128)S(1)} %get-tuple-element.8, bf16[128,896]{1,0:T(8,128)(2,1)S(1)} %collective-permute-done.7, bf16[128,896]{1,0:T(8,128)(2,1)S(1)} %collective-permute-done.6, bf16[128,896]{1,0:T(8,128)(2,1)S(1)} %collective-permute-done.5), kind=kLoop, calls=%fused_computation.8 | loop fusion | flops 802816 | bytes 1376256 | tf_op jit(solution)/shard_map/convert_element_type | solution.py:264
  (27 shorter events, 0.2 us)
Async XLA Ops:
  0.0 11.7 %copy-start = (s32[4]{0:T(128)S(1)}, s32[4]{0:T(128)}, u32[]{:S(2)}) copy-start(s32[4]{0:T(128)} %param.14) | copy-start | bytes 52
  1.1 13.9 %copy-start.1 = (bf16[128,576]{1,0:T(8,128)(2,1)}, bf16[128,576]{1,0:T(8,128)(2,1)S(1)}, u32[]{:S(2)}) copy-start(bf16[128,576]{1,0:T(8,128)(2,1)S(1)} %copy.15.group_ref) | copy-start | bytes 442372
  1.9 20.1 %collective-permute-start.2 = (bf16[80,576]{1,0:T(8,128)(2,1)S(1)}, bf16[80,576]{1,0:T(8,128)(2,1)S(1)}, u32[]{:S(2)}, u32[]{:S(2)}) collective-permute-start(bf16[80,576]{1,0:T(8,128)(2,1)S(1)} %pad_maximum_fusion.3), channel_id=1, source_target_pairs={{0,24},{8,0},{16,8},{24,16},{1,25},{9,1},{17,9},{25,17},{2,26},{10... | collective-permute-start | bytes 276488 | tf_op jit(solution)/shard_map/ppermute | solution.py:199
  7.0 15.0 %collective-permute-start.1 = (bf16[80,576]{1,0:T(8,128)(2,1)S(1)}, bf16[80,576]{1,0:T(8,128)(2,1)S(1)}, u32[]{:S(2)}, u32[]{:S(2)}) collective-permute-start(bf16[80,576]{1,0:T(8,128)(2,1)S(1)} %pad_maximum_fusion.3), channel_id=1, source_target_pairs={{0,16},{8,24},{16,0},{24,8},{1,17},{9,25},{17,1},{25,9},{2,18},{10... | collective-permute-start | bytes 276488 | tf_op jit(solution)/shard_map/ppermute | solution.py:199
  7.0 15.0 %collective-permute-start = (bf16[80,576]{1,0:T(8,128)(2,1)S(1)}, bf16[80,576]{1,0:T(8,128)(2,1)S(1)}, u32[]{:S(2)}, u32[]{:S(2)}) collective-permute-start(bf16[80,576]{1,0:T(8,128)(2,1)S(1)} %pad_maximum_fusion.3), channel_id=1, source_target_pairs={{0,8},{8,16},{16,24},{24,0},{1,9},{9,17},{17,25},{25,1},{2,10},{10... | collective-permute-start | bytes 276488 | tf_op jit(solution)/shard_map/ppermute | solution.py:199
  22.1 8.2 %copy-start.2 = (bf16[3,80,576]{2,1,0:T(8,128)(2,1)}, bf16[3,80,576]{2,1,0:T(8,128)(2,1)S(1)}, u32[]{:S(2)}) copy-start(bf16[3,80,576]{2,1,0:T(8,128)(2,1)S(1)} %pad_maximum_fusion.2.mine_ref) | copy-start | bytes 829444
  22.1 8.7 %collective-permute-start.3 = (bf16[3,80,576]{2,1,0:T(8,128)(2,1)S(1)}, bf16[3,80,576]{2,1,0:T(8,128)(2,1)S(1)}, u32[]{:S(2)}, u32[]{:S(2)}) collective-permute-start(bf16[3,80,576]{2,1,0:T(8,128)(2,1)S(1)} %pad_maximum_fusion.2.mine_ref), channel_id=1, source_target_pairs={{0,1},{1,0},{2,3},{3,2},{4,5},{5,4},{6,7},{7,6},{8,9},{9,8},{10,11... | collective-permute-start | bytes 829448 | tf_op jit(solution)/shard_map/ppermute | solution.py:203
  30.8 0.7 copy-start.3
  49.7 9.0 %collective-permute-start.4 = (bf16[4,128,896]{2,1,0:T(8,128)(2,1)}, bf16[4,128,896]{2,1,0:T(8,128)(2,1)S(1)}, u32[]{:S(2)}, u32[]{:S(2)}) collective-permute-start(bf16[4,128,896]{2,1,0:T(8,128)(2,1)} %project.3), channel_id=1, source_target_pairs={{0,1},{1,0},{2,3},{3,2},{4,5},{5,4},{6,7},{7,6},{8,9},{9,8},{10,11... | collective-permute-start | bytes 2752520 | tf_op jit(solution)/shard_map/ppermute | solution.py:255
  60.2 9.5 %collective-permute-start.5 = (bf16[128,896]{1,0:T(8,128)(2,1)S(1)}, bf16[128,896]{1,0:T(8,128)(2,1)S(1)}, u32[]{:S(2)}, u32[]{:S(2)}) collective-permute-start(bf16[128,896]{1,0:T(8,128)(2,1)S(1)} %get-tuple-element.9), channel_id=1, source_target_pairs={{0,6},{1,7},{2,4},{3,5},{4,2},{5,3},{6,0},{7,1},{8,14},{9,15},{10,... | collective-permute-start | bytes 688136 | tf_op jit(solution)/shard_map/ppermute | solution.py:260
  62.7 11.0 %collective-permute-start.7 = (bf16[128,896]{1,0:T(8,128)(2,1)S(1)}, bf16[128,896]{1,0:T(8,128)(2,1)S(1)}, u32[]{:S(2)}, u32[]{:S(2)}) collective-permute-start(bf16[128,896]{1,0:T(8,128)(2,1)S(1)} %get-tuple-element.10), channel_id=1, source_target_pairs={{0,2},{1,3},{2,0},{3,1},{4,6},{5,7},{6,4},{7,5},{8,10},{9,11},{10,... | collective-permute-start | bytes 688136 | tf_op jit(solution)/shard_map/ppermute | solution.py:260
  63.2 10.6 %collective-permute-start.6 = (bf16[128,896]{1,0:T(8,128)(2,1)S(1)}, bf16[128,896]{1,0:T(8,128)(2,1)S(1)}, u32[]{:S(2)}, u32[]{:S(2)}) collective-permute-start(bf16[128,896]{1,0:T(8,128)(2,1)S(1)} %get-tuple-element.11), channel_id=1, source_target_pairs={{0,4},{1,5},{2,6},{3,7},{4,0},{5,1},{6,2},{7,3},{8,12},{9,13},{10,... | collective-permute-start | bytes 688136 | tf_op jit(solution)/shard_map/ppermute | solution.py:260

commit v2 on v0

v2 whole, which is shorter than its diff:
```python
import functools
import math

import jax
import jax.numpy as jnp
from jax import lax
from jax.experimental import pallas as pl
from jax.experimental.pallas import tpu as pltpu
from jax.sharding import PartitionSpec as P


LATENT = 512
ROPE = 64
NOPE = 128
VDIM = 128
HALF = ROPE // 2
ENTRIES = LATENT + ROPE
LANES = 128
WIDE = -(-ENTRIES // LANES) * LANES
HIDDEN = -1e30
LOG2E = 1.4426950408889634
STREAMS = 8
MIB = 1 << 20


def in_hbm(*arrays):
    return [pltpu.with_memory_space_constraint(array, pltpu.HBM) for array in arrays]


def pack_kernel(group_ref, cache_ref, out_ref):
    core = lax.axis_index("tp") % 2
    features = group_ref.shape[0] // 2
    slots = cache_ref.shape[0] // 2
    out_ref[:features] = group_ref[pl.ds(pl.multiple_of(core * features, 16), features)]
    rows = cache_ref[pl.ds(pl.multiple_of(core * slots, 16), slots)]
    for tile in range(WIDE // LANES):
        piece = rows[:, tile * LANES : (tile + 1) * LANES]
        if piece.shape[1] < LANES:
            pad = jnp.zeros((slots, LANES - piece.shape[1]), piece.dtype)
            piece = jnp.concatenate([piece, pad], 1)
        start = features + tile * slots
        out_ref[start : start + slots] = piece


def pack(group_t, cache):
    slots = cache.shape[0] // 2
    rows = group_t.shape[0] // 2 + slots * (WIDE // LANES)
    return pl.pallas_call(
        pack_kernel,
        out_shape=jax.ShapeDtypeStruct((rows, group_t.shape[1]), jnp.bfloat16),
        name="pack",
        compiler_params=pltpu.CompilerParams(vmem_limit_bytes=4 * MIB),
    )(*in_hbm(group_t, cache))


def stream(source, base, target, sems):
    rows = target.shape[0] // STREAMS
    return [
        pltpu.make_async_copy(
            source.at[pl.ds(base + k * rows, rows)], target.at[pl.ds(k * rows, rows)], sems.at[k]
        )
        for k in range(STREAMS)
    ]


def front_kernel(fetch, offset_ref, nope_hbm, rope_hbm, up_hbm, *refs):
    if fetch:
        weight_ref, out_ref, cos_ref, sin_ref, stage_ref, *refs = refs
        *refs, stream_sems = refs
    else:
        out_ref, cos_ref, sin_ref, *refs = refs
    nope_ref, rope_ref, up_ref, turn_ref, sems = refs
    heads, tokens, _ = out_ref.shape
    pair = LANES // ROPE
    loads = [
        pltpu.make_async_copy(source, target, sems.at[k])
        for k, (source, target) in enumerate(
            [(rope_hbm, rope_ref), (nope_hbm, nope_ref), (up_hbm, up_ref)]
        )
    ]
    for copy in loads:
        copy.start()
    if fetch:
        streams = stream(weight_ref, 0, stage_ref, stream_sems)
        for copy in streams:
            copy.start()
    shape = cos_ref.shape
    position = offset_ref[0] + lax.broadcasted_iota(jnp.int32, shape, 1)
    index = lax.broadcasted_iota(jnp.int32, shape, 0).astype(jnp.float32)
    frequency = jnp.exp(index * (-2.0 * math.log(10000.0) / ROPE))
    angle = position.astype(jnp.float32) * frequency
    cos_ref[...] = jnp.cos(angle)
    sin_ref[...] = jnp.sin(angle)
    mine = pl.ds(pl.multiple_of(lax.axis_index("ctx") * tokens, LANES), tokens)
    cosine = cos_ref[:, mine]
    sine = sin_ref[:, mine]
    turn_ref[...] = jnp.concatenate([cosine, cosine, -sine, sine], 0).T
    for copy in loads:
        copy.wait()

    @pl.loop(0, heads // pair)
    def _(group):
        nope_at = pl.multiple_of(group * pair * NOPE, LANES)
        rope_at = pl.multiple_of(group * pair * ROPE, LANES)
        ropes = rope_ref[:, pl.ds(rope_at, pair * ROPE)].astype(jnp.float32)
        nopes = nope_ref[:, pl.ds(nope_at, pair * NOPE)]
        for head in range(pair):
            nope = nopes[:, head * NOPE : (head + 1) * NOPE]
            latent = jnp.dot(
                nope, up_ref[group * pair + head], preferred_element_type=jnp.float32
            )
            out_ref[group * pair + head, :, :LATENT] = latent.astype(jnp.bfloat16)
            raw = ropes[:, head * ROPE : (head + 1) * ROPE]
            swapped = jnp.concatenate([raw[:, HALF:], raw[:, :HALF]], 1)
            turned = raw * turn_ref[:, :ROPE] + swapped * turn_ref[:, ROPE:]
            pad = jnp.zeros((tokens, WIDE - ENTRIES), jnp.float32)
            filled = jnp.concatenate([turned, pad], 1)
            out_ref[group * pair + head, :, LATENT:] = filled.astype(jnp.bfloat16)

    if fetch:
        for copy in streams:
            copy.wait()


def front(ctx_size, offset, q_nope, q_rope, up_key, weight):
    tokens = q_nope.shape[0]
    heads = up_key.shape[0]
    vmem = pl.BlockSpec(memory_space=pltpu.VMEM)
    hbm = pl.BlockSpec(memory_space=pltpu.HBM)
    table = pltpu.VMEM((HALF, ctx_size * tokens), jnp.float32)
    in_specs = [pl.BlockSpec(memory_space=pltpu.SMEM), hbm, hbm, hbm]
    out_shape = [pltpu.VMEM((heads, tokens, WIDE), jnp.bfloat16), table, table]
    scratch = [
        pltpu.VMEM(q_nope.shape, q_nope.dtype),
        pltpu.VMEM(q_rope.shape, q_rope.dtype),
        pltpu.VMEM(up_key.shape, up_key.dtype),
        pltpu.VMEM((tokens, 2 * ROPE), jnp.float32),
        pltpu.SemaphoreType.DMA((3,)),
    ]
    args = [offset, q_nope, q_rope, up_key]
    if weight is not None:
        in_specs.append(hbm)
        out_shape.append(pltpu.VMEM(weight[1], weight[0].dtype))
        scratch.append(pltpu.SemaphoreType.DMA((STREAMS,)))
        args.append(weight[0])
    return pl.pallas_call(
        functools.partial(front_kernel, weight is not None),
        in_specs=in_specs,
        out_specs=[vmem] * len(out_shape),
        out_shape=out_shape,
        scratch_shapes=scratch,
        name="front",
        compiler_params=pltpu.CompilerParams(vmem_limit_bytes=8 * MIB),
        cost_estimate=pl.CostEstimate(
            flops=2 * heads * tokens * NOPE * LATENT, bytes_accessed=36 * MIB, transcendentals=0
        ),
    )(args[0], *in_hbm(*args[1:]))


def attend_kernel(step, first, counts_ref, q_ref, mine_ref, theirs_ref, cache_ref, group_ref, *refs):
    if first is None:
        cos_ref, sin_ref, up_ref, out_ref, keys_ref, bias_ref, cached_ref = refs
    else:
        cos_ref, sin_ref, up_ref, weight_ref, out_ref, stage_ref, *refs = refs
        keys_ref, bias_ref, cached_ref, sems = refs
        streams = stream(weight_ref, first, stage_ref, sems)
        for copy in streams:
            copy.start()
    shifts = mine_ref.shape[0]
    size = shifts + 1
    slots, tokens = cache_ref.shape[0], group_ref.shape[1]
    features = ENTRIES // 2
    tiles = WIDE // LANES
    ctx = lax.axis_index("ctx")
    core = lax.axis_index("tp") % 2
    keys_ref[ENTRIES:] = jnp.zeros((WIDE - ENTRIES, keys_ref.shape[1]), jnp.bfloat16)
    cached_ref[:slots, :ENTRIES] = cache_ref[...].astype(jnp.float32)
    cached_ref[:, ENTRIES:] = jnp.zeros((size * slots, WIDE - ENTRIES), jnp.float32)
    keys_ref[:ENTRIES, :tokens] = group_ref[...]
    for shift in range(shifts):
        lanes = slice((shift + 1) * tokens, (shift + 2) * tokens)
        for side, part in ((core, mine_ref), (1 - core, theirs_ref)):
            start = pl.multiple_of(side * features, 16)
            keys_ref[pl.ds(start, features), lanes] = part[shift, :features]
            start = pl.multiple_of((shift + 1) * slots + side * (slots // 2), 16)
            for tile in range(tiles):
                base = features + tile * (slots // 2)
                piece = part[shift, base : base + slots // 2].astype(jnp.float32)
                cached_ref[pl.ds(start, slots // 2), tile * LANES : (tile + 1) * LANES] = piece
    row = lax.broadcasted_iota(jnp.int32, (tokens, tokens), 0)
    lane = lax.broadcasted_iota(jnp.int32, (tokens, tokens), 1)
    bias_ref[:, :tokens] = jnp.where(lane <= row, 0.0, HIDDEN)
    slot = lax.broadcasted_iota(jnp.int32, (tokens, size * slots), 1)
    limit = jnp.full(slot.shape, counts_ref[ctx], jnp.int32)
    for shift in range(size):
        owner = lax.rem(ctx - shift + size, size)
        lanes = slice(shift * tokens, (shift + 1) * tokens)
        if shift > 0:
            shown = jnp.where(owner < ctx, 0.0, HIDDEN)
            bias_ref[:, lanes] = jnp.full((tokens, tokens), shown, jnp.float32)
            limit = jnp.where(slot >= shift * slots, shift * slots + counts_ref[owner], limit)
        where = pl.ds(pl.multiple_of(owner * tokens, LANES), tokens)
        cosine = cos_ref[:, where]
        sine = sin_ref[:, where]
        ahead = keys_ref[LATENT : LATENT + HALF, lanes].astype(jnp.float32)
        behind = keys_ref[LATENT + HALF : ENTRIES, lanes].astype(jnp.float32)
        keys_ref[LATENT : LATENT + HALF, lanes] = (ahead * cosine - behind * sine).astype(
            jnp.bfloat16
        )
        keys_ref[LATENT + HALF : ENTRIES, lanes] = (behind * cosine + ahead * sine).astype(
            jnp.bfloat16
        )
    bias_ref[:, size * tokens :] = jnp.where(slot < limit, 0.0, HIDDEN)
    keys_ref[:, size * tokens :] = cached_ref[...].T.astype(jnp.bfloat16)

    width = q_ref.shape[2]
    scale = LOG2E / math.sqrt(NOPE + ROPE)

    @pl.loop(0, q_ref.shape[0] // step)
    def _(group):
        queries = q_ref[pl.ds(group * step, step)].reshape(step * tokens, width)
        scores = jnp.dot(queries, keys_ref[...], preferred_element_type=jnp.float32)
        scores = scores.reshape(step, tokens, -1) + bias_ref[...][None]
        peak = jnp.max(scores, axis=2, keepdims=True)
        expos = jnp.exp2((scores - peak) * scale)
        total = jnp.sum(expos, axis=2, keepdims=True)
        weights = expos.astype(jnp.bfloat16).reshape(step * tokens, -1)
        mixed = lax.dot_general(
            weights, keys_ref[:LATENT], (((1,), (1,)), ((), ())), preferred_element_type=jnp.float32
        )
        attended = (mixed.reshape(step, tokens, LATENT) / total).astype(jnp.bfloat16)
        values = [
            jnp.dot(attended[head], up_ref[group * step + head], preferred_element_type=jnp.float32)
            for head in range(step)
        ]
        lanes = pl.ds(pl.multiple_of(group * step * VDIM, LANES), step * VDIM)
        out_ref[:, lanes] = jnp.concatenate(values, 1).astype(jnp.bfloat16)

    if first is not None:
        for copy in streams:
            copy.wait()


def attend(counts, queries, mine, theirs, cache, group_t, cosine, sine, up_value, weight, base):
    heads, tokens, width = queries.shape
    size = mine.shape[0] + 1
    slots = cache.shape[0]
    total = size * (tokens + slots)
    step = heads
    while step > 1 and step * tokens * total * 4 > 3 * MIB // 2:
        step //= 2
    vmem = pl.BlockSpec(memory_space=pltpu.VMEM)
    in_specs = [pl.BlockSpec(memory_space=pltpu.SMEM)] + [vmem] * 8
    out_shape = [pltpu.VMEM((tokens, heads * VDIM), jnp.bfloat16)]
    scratch = [
        pltpu.VMEM((WIDE, total), jnp.bfloat16),
        pltpu.VMEM((tokens, total), jnp.float32),
        pltpu.VMEM((size * slots, WIDE), jnp.float32),
    ]
    args = [counts, queries, mine, theirs, cache, group_t, cosine, sine, up_value]
    if base is not None:
        in_specs.append(pl.BlockSpec(memory_space=pltpu.HBM))
        out_shape.append(pltpu.VMEM((weight.shape[0] - base, weight.shape[1]), weight.dtype))
        scratch.append(pltpu.SemaphoreType.DMA((STREAMS,)))
        args += in_hbm(weight)
    return pl.pallas_call(
        functools.partial(attend_kernel, step, base),
        in_specs=in_specs,
        out_specs=[vmem] * len(out_shape),
        out_shape=out_shape,
        scratch_shapes=scratch,
        name="attend",
        compiler_params=pltpu.CompilerParams(vmem_limit_bytes=10 * MIB + total * 8192),
        cost_estimate=pl.CostEstimate(
            flops=2 * heads * tokens * total * (LATENT + width),
            bytes_accessed=8 * MIB,
            transcendentals=heads * tokens * total,
        ),
    )(*args)


def project_kernel(width, deltas, theirs, add, head_ref, upper_ref, lower_ref, *refs):
    tp = lax.axis_index("tp")
    side = 1 - tp % 2 if theirs else tp % 2
    count = len(deltas)
    outs = refs[count if add else 0 :]
    for place, delta in enumerate(deltas):
        start = pl.multiple_of((((tp // 2) ^ delta) * 2 + side) * width, LANES)
        lanes = pl.ds(start, width)
        split = upper_ref.shape[0]
        block = jnp.dot(
            head_ref[:, :split], upper_ref[:, lanes], preferred_element_type=jnp.float32
        ) + jnp.dot(head_ref[:, split:], lower_ref[:, lanes], preferred_element_type=jnp.float32)
        if add:
            block = block + refs[place][...].astype(jnp.float32)
        outs[place][...] = block.astype(jnp.bfloat16)


def project(head_out, upper, lower, width, deltas, theirs, arrived=()):
    tokens, depth = head_out.shape
    out = jax.ShapeDtypeStruct((tokens, width), jnp.bfloat16)
    return pl.pallas_call(
        functools.partial(project_kernel, width, deltas, theirs, bool(arrived)),
        in_specs=[pl.BlockSpec(memory_space=pltpu.VMEM)] * (3 + len(arrived)),
        out_specs=[pl.BlockSpec(memory_space=pltpu.VMEM)] * len(deltas),
        out_shape=[out] * len(deltas),
        name="project",
        compiler_params=pltpu.CompilerParams(vmem_limit_bytes=6 * MIB),
        cost_estimate=pl.CostEstimate(
            flops=2 * len(deltas) * tokens * depth * width,
            bytes_accessed=2 * len(deltas) * tokens * width,
            transcendentals=0,
        ),
    )(head_out, upper, lower, *arrived)


def layer(
    ctx_size, tp_size, q_nope, q_rope, cache_latent, group_latent, offset, counts, up_key, up_value,
    out_weight,
):
    width = out_weight.shape[1] // tp_size
    chips = tp_size // 2
    direct = width % LANES == 0 and chips & (chips - 1) == 0
    swap = [(i, i ^ 1) for i in range(tp_size)]

    group_t = group_latent.T
    part = pack(group_t, cache_latent)
    arrived = []
    for shift in range(1, ctx_size):
        ring = [(i, (i + shift) % ctx_size) for i in range(ctx_size)]
        arrived.append(lax.ppermute(part, "ctx", ring))
    mine = jnp.stack(arrived)
    theirs = lax.ppermute(mine, "tp", swap)
    depth, columns = out_weight.shape
    base = depth // 2 if direct else None
    weight = (out_weight, (base, columns)) if direct else None
    queries, cosine, sine, *upper = front(ctx_size, offset, q_nope, q_rope, up_key, weight)
    head_out, *lower = attend(
        counts, queries, mine, theirs, cache_latent, group_t, cosine, sine, up_value, out_weight,
        base,
    )
    if not direct:
        partial = jnp.dot(head_out, out_weight, preferred_element_type=jnp.float32)
        summed = lax.psum_scatter(
            partial.astype(jnp.bfloat16), "tp", scatter_dimension=1, tiled=True
        )
        return summed.astype(jnp.bfloat16)

    groups = [[chips - 1], list(range(1, chips - 1)), [0]]
    arrived = []
    for deltas in groups:
        sent = project(head_out, upper[0], lower[0], width, deltas, True)
        arrived.append([lax.ppermute(block, "tp", swap) for block in sent])
    moved = []
    for deltas, blocks in zip(groups, arrived):
        sums = project(head_out, upper[0], lower[0], width, deltas, False, tuple(blocks))
        for delta, block in zip(deltas, sums):
            if delta:
                block = lax.ppermute(block, "tp", [(i, i ^ (2 * delta)) for i in range(tp_size)])
            moved.append(block.astype(jnp.float32))
    return sum(moved).astype(jnp.bfloat16)


def solution(mesh):
    return jax.shard_map(
        functools.partial(layer, mesh.shape["ctx"], mesh.shape["tp"]),
        mesh=mesh,
        in_specs=(
            P("ctx", "tp"),
            P("ctx", "tp"),
            P("ctx", None),
            P("ctx", None),
            P(),
            P(),
            P("tp", None, None),
            P("tp", None, None),
            P("tp", None),
        ),
        out_specs=P("ctx", "tp"),
        check_vma=False,
    )
```

time: 128 us -> 49.5 us (0.39)
  matrix products: 27.4 us -> 0 us
  waiting for transfers between devices: 39.3 us -> 15.7 us
  blocking collectives: 22.1 us -> 0 us
  Pallas kernels: 0 us -> 20.6 us
  between operations: 14.9 us -> 0.78 us
  local copies, waits for them, and re-layouts: 14.2 us -> 0.26 us
  starting transfers between devices: 0.01 us -> 11.1 us
  other arithmetic: 9.85 us -> 0.85 us
    unnamed x2 -> x0, waiting for transfers between devices: 39.3 us -> none
    dot_general x5 -> x0, matrix products: 27.4 us -> none  [the longest x1 14.8 us: local(): lax.dot_general(out_weight, head_out, (((0,), (1,)), ((), ())), preferred...]
    all_gather x1 -> x0, blocking collectives: 22.1 us -> none  [local(): key_block = lax.all_gather(local_keys, 'ctx', axis=0, tiled=True)]
    pallas_call x0 -> x9, Pallas kernels: none -> 20.6 us  [the longest x1 7.72 us: attend(): pl.pallas_call(functools.partial(attend_kernel, step, base), in_specs=in_...]
    ppermute x0 -> x11, waiting for transfers between devices: none -> 15.7 us  [the longest x3 8.2 us: layer(): lax.ppermute(block, 'tp', [(i, i ^ 2 * delta) for i in range(tp_size)])]
    ppermute x0 -> x11, starting transfers between devices: none -> 11.1 us  [the longest x3 6.14 us: layer(): arrived.append(lax.ppermute(part, 'ctx', ring))]
    unnamed x10 -> x8, local copies, waits for them, and re-layouts: 7.73 us -> 0.26 us
    another operation x3 -> x0, local copies, waits for them, and re-layouts: 5.15 us -> none
  transfers between devices with their start and end apart: 1 -> 11, of which waited for: 1 -> 4; matrix products, arithmetic and copies ran while one was open for 0% -> 0% of each run, Pallas kernels for 0% -> 23%
where the time goes in v2:
time: 49.5 us; the launch traced here: 49.3 us
  Pallas kernels  20.6 us (42%)
  waiting for transfers between devices  15.7 us (32%)
  starting transfers between devices  11.1 us (22%)
  other arithmetic  0.85 us (2%)
  between operations  0.78 us (2%)
    ppermute x3, waiting for transfers between devices, layer(): lax.ppermute(block, 'tp', [(i, i ^ 2 * delta) for i in range(tp_size)])  8.2 us
    pallas_call x1, Pallas kernels, attend(): pl.pallas_call(functools.partial(attend_kernel, step, base), in_specs=in_...  7.72 us
    ppermute x3, waiting for transfers between devices, layer(): arrived.append(lax.ppermute(part, 'ctx', ring))  7.44 us
    pallas_call x1, Pallas kernels, front(): pl.pallas_call(functools.partial(front_kernel, weight is not None), in_sp...  6.36 us
    ppermute x3, starting transfers between devices, layer(): arrived.append(lax.ppermute(part, 'ctx', ring))  6.14 us
    pallas_call x6, Pallas kernels, project(): pl.pallas_call(functools.partial(project_kernel, width, deltas, theirs, b...  5.64 us
    ppermute x3, starting transfers between devices, layer(): lax.ppermute(block, 'tp', [(i, i ^ 2 * delta) for i in range(tp_size)])  3.63 us
    ppermute x4, starting transfers between devices, layer(): arrived.append([lax.ppermute(block, 'tp', swap) for block in sent])  1.28 us
  transfers between devices with their start and end apart: 11, of which 4 were waited for; matrix products, arithmetic and copies ran while one was open for 0% of the time, Pallas kernels for 23%

profile of v2, /device:TPU:0, one launch (start us, length us, event | category | flops | bytes accessed | tf_op | source)
XLA Modules:
  0.0 49.3 jit_solution(10852288057391704467)
XLA Ops:
  0.0 0.9 %pack.1 = bf16[368,128]{1,0:T(8,128)(2,1)S(1)} custom-call(bf16[576,128]{1,0:T(8,128)(2,1)} %bitcast.4, bf16[32,576]{1,0:T(8,128)(2,1)} %cache_ref.3), custom_call_target="tpu_custom_call" | custom-call | tf_op jit(solution)/shard_map/pack/pallas_call | solution.py:48
  0.9 5.1 %collective-permute-start.2 = (bf16[368,128]{1,0:T(8,128)(2,1)S(1)}, bf16[368,128]{1,0:T(8,128)(2,1)S(1)}, u32[]{:S(2)}, u32[]{:S(2)}) collective-permute-start(bf16[368,128]{1,0:T(8,128)(2,1)S(1)} %pack.1), channel_id=1, source_target_pairs={{0,24},{8,0},{16,8},{24,16},{1,25},{9,1},{17,9},{25,17},{2,26},{10... | collective-permute-start | bytes 282632 | tf_op jit(solution)/shard_map/ppermute | solution.py:331
  6.1 0.0 collective-permute-start.1
  6.1 1.0 %collective-permute-start = (bf16[368,128]{1,0:T(8,128)(2,1)S(1)}, bf16[368,128]{1,0:T(8,128)(2,1)S(1)}, u32[]{:S(2)}, u32[]{:S(2)}) collective-permute-start(bf16[368,128]{1,0:T(8,128)(2,1)S(1)} %pack.1), channel_id=1, source_target_pairs={{0,8},{8,16},{16,24},{24,0},{1,9},{9,17},{17,25},{25,1},{2,10},{10... | collective-permute-start | bytes 282632 | tf_op jit(solution)/shard_map/ppermute | solution.py:331
  7.1 2.1 %collective-permute-done.2 = bf16[368,128]{1,0:T(8,128)(2,1)S(1)} collective-permute-done((bf16[368,128]{1,0:T(8,128)(2,1)S(1)}, bf16[368,128]{1,0:T(8,128)(2,1)S(1)}, u32[]{:S(2)}, u32[]{:S(2)}) %collective-permute-start.2) | collective-permute-done | bytes 94240 | tf_op jit(solution)/shard_map/ppermute | solution.py:331
  9.2 5.4 %collective-permute-done.1 = bf16[368,128]{1,0:T(8,128)(2,1)S(1)} collective-permute-done((bf16[368,128]{1,0:T(8,128)(2,1)S(1)}, bf16[368,128]{1,0:T(8,128)(2,1)S(1)}, u32[]{:S(2)}, u32[]{:S(2)}) %collective-permute-start.1) | collective-permute-done | bytes 94240 | tf_op jit(solution)/shard_map/ppermute | solution.py:331
  14.5 0.0 collective-permute-done
  14.5 0.1 collective-permute-start.3
  15.3 0.0 copy-start
  15.3 0.0 copy-start.1
  15.3 0.0 copy-start.2
  15.3 0.0 copy-start.3
  15.3 6.4 %front.1 = (bf16[16,128,640]{2,1,0:T(8,128)(2,1)S(1)}, f32[32,512]{1,0:T(8,128)S(1)}, f32[32,512]{1,0:T(8,128)S(1)}, bf16[1024,7168]{1,0:T(8,128)(2,1)S(1)}) custom-call(s32[1]{0:T(128)S(6)} %copy.10.offset_ref, bf16[128,2048]{1,0:T(8,128)(2,1)} %nope_hbm.1, bf16[128,1024]{1,0:T(8,128)(2,1)} %rope_hbm.1, bf16[16,128,512]{2,1,0:T(8,128)(2,1)} %up_hbm.1, ...), custom_call_target="tpu_custom_call" | custom-call | flops 268435456 | bytes 37748736 | tf_op jit(solution)/shard_map/front/pallas_call | solution.py:146
  21.7 0.0 collective-permute-done.3.theirs_ref
  21.7 0.2 copy-done
  21.9 0.0 copy-done.1
  21.9 0.0 copy-done.2
  21.9 0.0 copy-done.3
  21.9 7.7 %attend.1 = (bf16[128,2048]{1,0:T(8,128)(2,1)S(1)}, bf16[1024,7168]{1,0:T(8,128)(2,1)S(1)}) custom-call(s32[4]{0:T(128)S(1)} %copy-done.3, bf16[16,128,640]{2,1,0:T(8,128)(2,1)S(1)} %get-tuple-element.15.q_ref, bf16[3,368,128]{2,1,0:T(8,128)(2,1)S(1)} %pad_maximum_fusion.mine_ref, bf16[3,368,128]{2,1,0:T(8,128)(2,1)S(1)} %collective-permute-done.3.theirs_ref, ...), custom_call_target="tpu_custom_call" | custom-call | flops 3019898880 | bytes 8388608 | tf_op jit(solution)/shard_map/attend/pallas_call | solution.py:266
  29.7 0.8 %project.6 = bf16[128,896]{1,0:T(8,128)(2,1)S(1)} custom-call(bf16[128,2048]{1,0:T(8,128)(2,1)S(1)} %get-tuple-element.18.head_ref, bf16[1024,7168]{1,0:T(8,128)(2,1)S(1)} %get-tuple-element.19.upper_ref, bf16[1024,7168]{1,0:T(8,128)(2,1)S(1)} %get-tuple-element.20.lower_ref), custom_call_target="tpu_custom_call" | custom-call | flops 469762048 | bytes 229376 | tf_op jit(solution)/shard_map/project/pallas_call | solution.py:302
  30.5 0.6 %collective-permute-start.4 = (bf16[128,896]{1,0:T(8,128)(2,1)S(1)}, bf16[128,896]{1,0:T(8,128)(2,1)S(1)}, u32[]{:S(2)}, u32[]{:S(2)}) collective-permute-start(bf16[128,896]{1,0:T(8,128)(2,1)S(1)} %project.6), channel_id=1, source_target_pairs={{0,1},{1,0},{2,3},{3,2},{4,5},{5,4},{6,7},{7,6},{8,9},{9,8},{10,11... | collective-permute-start | bytes 688136 | tf_op jit(solution)/shard_map/ppermute | solution.py:353
  31.0 1.3 %project.8 = (bf16[128,896]{1,0:T(8,128)(2,1)S(1)}, bf16[128,896]{1,0:T(8,128)(2,1)S(1)}) custom-call(bf16[128,2048]{1,0:T(8,128)(2,1)S(1)} %get-tuple-element.18.head_ref, bf16[1024,7168]{1,0:T(8,128)(2,1)S(1)} %get-tuple-element.19.upper_ref, bf16[1024,7168]{1,0:T(8,128)(2,1)S(1)} %get-tuple-element.20.lower_ref), custom_call_target="tpu_custom_call" | custom-call | flops 939524096 | bytes 458752 | tf_op jit(solution)/shard_map/project/pallas_call | solution.py:302
  32.4 0.1 collective-permute-start.6
  32.5 0.5 %collective-permute-start.7 = (bf16[128,896]{1,0:T(8,128)(2,1)S(1)}, bf16[128,896]{1,0:T(8,128)(2,1)S(1)}, u32[]{:S(2)}, u32[]{:S(2)}) collective-permute-start(bf16[128,896]{1,0:T(8,128)(2,1)S(1)} %get-tuple-element.22), channel_id=1, source_target_pairs={{0,1},{1,0},{2,3},{3,2},{4,5},{5,4},{6,7},{7,6},{8,9},{9,8},{10,11... | collective-permute-start | bytes 688136 | tf_op jit(solution)/shard_map/ppermute | solution.py:353
  32.9 0.7 %project.10 = bf16[128,896]{1,0:T(8,128)(2,1)S(1)} custom-call(bf16[128,2048]{1,0:T(8,128)(2,1)S(1)} %get-tuple-element.18.head_ref, bf16[1024,7168]{1,0:T(8,128)(2,1)S(1)} %get-tuple-element.19.upper_ref, bf16[1024,7168]{1,0:T(8,128)(2,1)S(1)} %get-tuple-element.20.lower_ref), custom_call_target="tpu_custom_call" | custom-call | flops 469762048 | bytes 229376 | tf_op jit(solution)/shard_map/project/pallas_call | solution.py:302
  33.7 0.1 collective-permute-start.10
  33.8 0.0 collective-permute-done.4.refs_0_
  33.8 0.8 %project.7 = bf16[128,896]{1,0:T(8,128)(2,1)S(1)} custom-call(bf16[128,2048]{1,0:T(8,128)(2,1)S(1)} %get-tuple-element.18.head_ref, bf16[1024,7168]{1,0:T(8,128)(2,1)S(1)} %get-tuple-element.19.upper_ref, bf16[1024,7168]{1,0:T(8,128)(2,1)S(1)} %get-tuple-element.20.lower_ref, bf16[128,896]{1,0:T(8,128)(2,1)S(1)} %collective-permute-done.4.refs_0_), custom_call_target="tpu_custom_call" | custom-call | flops 469762048 | bytes 229376 | tf_op jit(solution)/shard_map/project/pallas_call | solution.py:302
  34.6 2.5 %collective-permute-start.5 = (bf16[128,896]{1,0:T(8,128)(2,1)S(1)}, bf16[128,896]{1,0:T(8,128)(2,1)S(1)}, u32[]{:S(2)}, u32[]{:S(2)}) collective-permute-start(bf16[128,896]{1,0:T(8,128)(2,1)S(1)} %project.7), channel_id=1, source_target_pairs={{0,6},{1,7},{2,4},{3,5},{4,2},{5,3},{6,0},{7,1},{8,14},{9,15},{10,... | collective-permute-start | bytes 688136 | tf_op jit(solution)/shard_map/ppermute | solution.py:359
  37.1 0.0 collective-permute-done.6.refs_0_
  37.1 0.0 collective-permute-done.7.refs_1_
  37.1 1.3 %project.9 = (bf16[128,896]{1,0:T(8,128)(2,1)S(1)}, bf16[128,896]{1,0:T(8,128)(2,1)S(1)}) custom-call(bf16[128,2048]{1,0:T(8,128)(2,1)S(1)} %get-tuple-element.18.head_ref, bf16[1024,7168]{1,0:T(8,128)(2,1)S(1)} %get-tuple-element.19.upper_ref, bf16[1024,7168]{1,0:T(8,128)(2,1)S(1)} %get-tuple-element.20.lower_ref, ...), custom_call_target="tpu_custom_call" | custom-call | flops 939524096 | bytes 458752 | tf_op jit(solution)/shard_map/project/pallas_call | solution.py:302
  38.4 0.6 %collective-permute-start.8 = (bf16[128,896]{1,0:T(8,128)(2,1)S(1)}, bf16[128,896]{1,0:T(8,128)(2,1)S(1)}, u32[]{:S(2)}, u32[]{:S(2)}) collective-permute-start(bf16[128,896]{1,0:T(8,128)(2,1)S(1)} %get-tuple-element.23), channel_id=1, source_target_pairs={{0,2},{1,3},{2,0},{3,1},{4,6},{5,7},{6,4},{7,5},{8,10},{9,11},{10,... | collective-permute-start | bytes 688136 | tf_op jit(solution)/shard_map/ppermute | solution.py:359
  39.0 0.6 %collective-permute-start.9 = (bf16[128,896]{1,0:T(8,128)(2,1)S(1)}, bf16[128,896]{1,0:T(8,128)(2,1)S(1)}, u32[]{:S(2)}, u32[]{:S(2)}) collective-permute-start(bf16[128,896]{1,0:T(8,128)(2,1)S(1)} %get-tuple-element.24), channel_id=1, source_target_pairs={{0,4},{1,5},{2,6},{3,7},{4,0},{5,1},{6,2},{7,3},{8,12},{9,13},{10,... | collective-permute-start | bytes 688136 | tf_op jit(solution)/shard_map/ppermute | solution.py:359
  39.5 0.0 collective-permute-done.10.refs_0_
  39.6 0.7 %project.11 = bf16[128,896]{1,0:T(8,128)(2,1)S(1)} custom-call(bf16[128,2048]{1,0:T(8,128)(2,1)S(1)} %get-tuple-element.18.head_ref, bf16[1024,7168]{1,0:T(8,128)(2,1)S(1)} %get-tuple-element.19.upper_ref, bf16[1024,7168]{1,0:T(8,128)(2,1)S(1)} %get-tuple-element.20.lower_ref, bf16[128,896]{1,0:T(8,128)(2,1)S(1)} %collective-permute-done.10.refs_0_), custom_call_target="tpu_custom_call" | custom-call | flops 469762048 | bytes 229376 | tf_op jit(solution)/shard_map/project/pallas_call | solution.py:302
  40.3 3.7 %collective-permute-done.5 = bf16[128,896]{1,0:T(8,128)(2,1)S(1)} collective-permute-done((bf16[128,896]{1,0:T(8,128)(2,1)S(1)}, bf16[128,896]{1,0:T(8,128)(2,1)S(1)}, u32[]{:S(2)}, u32[]{:S(2)}) %collective-permute-start.5) | collective-permute-done | bytes 229408 | tf_op jit(solution)/shard_map/ppermute | solution.py:359
  44.0 4.5 %collective-permute-done.8 = bf16[128,896]{1,0:T(8,128)(2,1)S(1)} collective-permute-done((bf16[128,896]{1,0:T(8,128)(2,1)S(1)}, bf16[128,896]{1,0:T(8,128)(2,1)S(1)}, u32[]{:S(2)}, u32[]{:S(2)}) %collective-permute-start.8) | collective-permute-done | bytes 229408 | tf_op jit(solution)/shard_map/ppermute | solution.py:359
  48.5 0.0 collective-permute-done.9
  48.5 0.8 %add_convert_fusion = bf16[128,896]{1,0:T(8,128)(2,1)} fusion(bf16[128,896]{1,0:T(8,128)(2,1)S(1)} %project.11, bf16[128,896]{1,0:T(8,128)(2,1)S(1)} %collective-permute-done.9, bf16[128,896]{1,0:T(8,128)(2,1)S(1)} %collective-permute-done.8, bf16[128,896]{1,0:T(8,128)(2,1)S(1)} %collective-permute-done.5), kind=kLoop, calls=%fused_computation | loop fusion | flops 917504 | bytes 1146880 | tf_op jit(solution)/shard_map/convert_element_type | solution.py:361
  (1 shorter events, 0.0 us)
Async XLA Ops:
  0.9 8.2 %collective-permute-start.2 = (bf16[368,128]{1,0:T(8,128)(2,1)S(1)}, bf16[368,128]{1,0:T(8,128)(2,1)S(1)}, u32[]{:S(2)}, u32[]{:S(2)}) collective-permute-start(bf16[368,128]{1,0:T(8,128)(2,1)S(1)} %pack.1), channel_id=1, source_target_pairs={{0,24},{8,0},{16,8},{24,16},{1,25},{9,1},{17,9},{25,17},{2,26},{10... | collective-permute-start | bytes 282632 | tf_op jit(solution)/shard_map/ppermute | solution.py:331
  6.1 8.4 %collective-permute-start.1 = (bf16[368,128]{1,0:T(8,128)(2,1)S(1)}, bf16[368,128]{1,0:T(8,128)(2,1)S(1)}, u32[]{:S(2)}, u32[]{:S(2)}) collective-permute-start(bf16[368,128]{1,0:T(8,128)(2,1)S(1)} %pack.1), channel_id=1, source_target_pairs={{0,16},{8,24},{16,0},{24,8},{1,17},{9,25},{17,1},{25,9},{2,18},{10... | collective-permute-start | bytes 282632 | tf_op jit(solution)/shard_map/ppermute | solution.py:331
  6.1 8.4 %collective-permute-start = (bf16[368,128]{1,0:T(8,128)(2,1)S(1)}, bf16[368,128]{1,0:T(8,128)(2,1)S(1)}, u32[]{:S(2)}, u32[]{:S(2)}) collective-permute-start(bf16[368,128]{1,0:T(8,128)(2,1)S(1)} %pack.1), channel_id=1, source_target_pairs={{0,8},{8,16},{16,24},{24,0},{1,9},{9,17},{17,25},{25,1},{2,10},{10... | collective-permute-start | bytes 282632 | tf_op jit(solution)/shard_map/ppermute | solution.py:331
  14.5 7.1 %collective-permute-start.3 = (bf16[3,368,128]{2,1,0:T(8,128)(2,1)S(1)}, bf16[3,368,128]{2,1,0:T(8,128)(2,1)S(1)}, u32[]{:S(2)}, u32[]{:S(2)}) collective-permute-start(bf16[3,368,128]{2,1,0:T(8,128)(2,1)S(1)} %pad_maximum_fusion.mine_ref), channel_id=1, source_target_pairs={{0,1},{1,0},{2,3},{3,2},{4,5},{5,4},{6,7},{7,6},{8,9},{9,8},{10,11... | collective-permute-start | bytes 847880 | tf_op jit(solution)/shard_map/ppermute | solution.py:333
  15.3 6.7 %copy-start = (bf16[16,512,128]{2,1,0:T(8,128)(2,1)S(1)}, bf16[16,512,128]{2,1,0:T(8,128)(2,1)}, u32[]{:S(2)}) copy-start(bf16[16,512,128]{2,1,0:T(8,128)(2,1)} %refs_2_.1) | copy-start | bytes 6291460
  15.3 6.7 %copy-start.1 = (bf16[128,576]{0,1:T(8,128)(2,1)S(1)}, bf16[128,576]{0,1:T(8,128)(2,1)}, u32[]{:S(2)}) copy-start(bf16[128,576]{0,1:T(8,128)(2,1)} %param.12) | copy-start | bytes 442372
  15.3 6.6 %copy-start.2 = (bf16[32,576]{1,0:T(8,128)(2,1)S(1)}, bf16[32,576]{1,0:T(8,128)(2,1)}, u32[]{:S(2)}) copy-start(bf16[32,576]{1,0:T(8,128)(2,1)} %cache_ref.3) | copy-start | bytes 110596
  15.3 6.6 %copy-start.3 = (s32[4]{0:T(128)S(1)}, s32[4]{0:T(128)}, u32[]{:S(2)}) copy-start(s32[4]{0:T(128)} %counts_ref.1) | copy-start | bytes 52
  30.5 3.4 %collective-permute-start.4 = (bf16[128,896]{1,0:T(8,128)(2,1)S(1)}, bf16[128,896]{1,0:T(8,128)(2,1)S(1)}, u32[]{:S(2)}, u32[]{:S(2)}) collective-permute-start(bf16[128,896]{1,0:T(8,128)(2,1)S(1)} %project.6), channel_id=1, source_target_pairs={{0,1},{1,0},{2,3},{3,2},{4,5},{5,4},{6,7},{7,6},{8,9},{9,8},{10,11... | collective-permute-start | bytes 688136 | tf_op jit(solution)/shard_map/ppermute | solution.py:353
  32.4 4.7 %collective-permute-start.6 = (bf16[128,896]{1,0:T(8,128)(2,1)S(1)}, bf16[128,896]{1,0:T(8,128)(2,1)S(1)}, u32[]{:S(2)}, u32[]{:S(2)}) collective-permute-start(bf16[128,896]{1,0:T(8,128)(2,1)S(1)} %get-tuple-element.21), channel_id=1, source_target_pairs={{0,1},{1,0},{2,3},{3,2},{4,5},{5,4},{6,7},{7,6},{8,9},{9,8},{10,11... | collective-permute-start | bytes 688136 | tf_op jit(solution)/shard_map/ppermute | solution.py:353
  32.5 4.6 %collective-permute-start.7 = (bf16[128,896]{1,0:T(8,128)(2,1)S(1)}, bf16[128,896]{1,0:T(8,128)(2,1)S(1)}, u32[]{:S(2)}, u32[]{:S(2)}) collective-permute-start(bf16[128,896]{1,0:T(8,128)(2,1)S(1)} %get-tuple-element.22), channel_id=1, source_target_pairs={{0,1},{1,0},{2,3},{3,2},{4,5},{5,4},{6,7},{7,6},{8,9},{9,8},{10,11... | collective-permute-start | bytes 688136 | tf_op jit(solution)/shard_map/ppermute | solution.py:353
  33.7 5.9 %collective-permute-start.10 = (bf16[128,896]{1,0:T(8,128)(2,1)S(1)}, bf16[128,896]{1,0:T(8,128)(2,1)S(1)}, u32[]{:S(2)}, u32[]{:S(2)}) collective-permute-start(bf16[128,896]{1,0:T(8,128)(2,1)S(1)} %project.10), channel_id=1, source_target_pairs={{0,1},{1,0},{2,3},{3,2},{4,5},{5,4},{6,7},{7,6},{8,9},{9,8},{10,11... | collective-permute-start | bytes 688136 | tf_op jit(solution)/shard_map/ppermute | solution.py:353
  34.6 9.4 %collective-permute-start.5 = (bf16[128,896]{1,0:T(8,128)(2,1)S(1)}, bf16[128,896]{1,0:T(8,128)(2,1)S(1)}, u32[]{:S(2)}, u32[]{:S(2)}) collective-permute-start(bf16[128,896]{1,0:T(8,128)(2,1)S(1)} %project.7), channel_id=1, source_target_pairs={{0,6},{1,7},{2,4},{3,5},{4,2},{5,3},{6,0},{7,1},{8,14},{9,15},{10,... | collective-permute-start | bytes 688136 | tf_op jit(solution)/shard_map/ppermute | solution.py:359
  38.4 10.1 %collective-permute-start.8 = (bf16[128,896]{1,0:T(8,128)(2,1)S(1)}, bf16[128,896]{1,0:T(8,128)(2,1)S(1)}, u32[]{:S(2)}, u32[]{:S(2)}) collective-permute-start(bf16[128,896]{1,0:T(8,128)(2,1)S(1)} %get-tuple-element.23), channel_id=1, source_target_pairs={{0,2},{1,3},{2,0},{3,1},{4,6},{5,7},{6,4},{7,5},{8,10},{9,11},{10,... | collective-permute-start | bytes 688136 | tf_op jit(solution)/shard_map/ppermute | solution.py:359
  39.0 9.5 %collective-permute-start.9 = (bf16[128,896]{1,0:T(8,128)(2,1)S(1)}, bf16[128,896]{1,0:T(8,128)(2,1)S(1)}, u32[]{:S(2)}, u32[]{:S(2)}) collective-permute-start(bf16[128,896]{1,0:T(8,128)(2,1)S(1)} %get-tuple-element.24), channel_id=1, source_target_pairs={{0,4},{1,5},{2,6},{3,7},{4,0},{5,1},{6,2},{7,3},{8,12},{9,13},{10,... | collective-permute-start | bytes 688136 | tf_op jit(solution)/shard_map/ppermute | solution.py:359

commit v3 on v2

--- a/solution.py
+++ b/solution.py
@@ -247,7 +247,7 @@
     slots = cache.shape[0]
     total = size * (tokens + slots)
     step = heads
-    while step > 1 and step * tokens * total * 4 > 3 * MIB // 2:
+    while step > 1 and step * tokens * total * 4 > 3 * MIB:
         step //= 2
     vmem = pl.BlockSpec(memory_space=pltpu.VMEM)
     in_specs = [pl.BlockSpec(memory_space=pltpu.SMEM)] + [vmem] * 8
@@ -279,31 +279,34 @@
     )(*args)
 
 
-def project_kernel(width, deltas, theirs, add, head_ref, upper_ref, lower_ref, *refs):
+def project_kernel(width, deltas, theirs, add, parts, head_ref, upper_ref, lower_ref, *refs):
     tp = lax.axis_index("tp")
     side = 1 - tp % 2 if theirs else tp % 2
-    count = len(deltas)
-    outs = refs[count if add else 0 :]
+    split = upper_ref.shape[0]
+    outs = refs[len(deltas) if add else 0 :]
     for place, delta in enumerate(deltas):
         start = pl.multiple_of((((tp // 2) ^ delta) * 2 + side) * width, LANES)
         lanes = pl.ds(start, width)
-        split = upper_ref.shape[0]
         block = jnp.dot(
             head_ref[:, :split], upper_ref[:, lanes], preferred_element_type=jnp.float32
         ) + jnp.dot(head_ref[:, split:], lower_ref[:, lanes], preferred_element_type=jnp.float32)
         if add:
             block = block + refs[place][...].astype(jnp.float32)
-        outs[place][...] = block.astype(jnp.bfloat16)
-
-
-def project(head_out, upper, lower, width, deltas, theirs, arrived=()):
+        block = block.astype(jnp.bfloat16)
+        rows = block.shape[0] // parts
+        for part in range(parts):
+            outs[place * parts + part][...] = block[part * rows : (part + 1) * rows]
+
+
+def project(head_out, upper, lower, width, deltas, theirs, arrived=(), parts=1):
     tokens, depth = head_out.shape
-    out = jax.ShapeDtypeStruct((tokens, width), jnp.bfloat16)
+    out = jax.ShapeDtypeStruct((tokens // parts, width), jnp.bfloat16)
+    count = len(deltas) * parts
     return pl.pallas_call(
-        functools.partial(project_kernel, width, deltas, theirs, bool(arrived)),
+        functools.partial(project_kernel, width, deltas, theirs, bool(arrived), parts),
         in_specs=[pl.BlockSpec(memory_space=pltpu.VMEM)] * (3 + len(arrived)),
-        out_specs=[pl.BlockSpec(memory_space=pltpu.VMEM)] * len(deltas),
-        out_shape=[out] * len(deltas),
+        out_specs=[pl.BlockSpec(memory_space=pltpu.VMEM)] * count,
+        out_shape=[out] * count,
         name="project",
         compiler_params=pltpu.CompilerParams(vmem_limit_bytes=6 * MIB),
         cost_estimate=pl.CostEstimate(
@@ -320,7 +323,7 @@
 ):
     width = out_weight.shape[1] // tp_size
     chips = tp_size // 2
-    direct = width % LANES == 0 and chips & (chips - 1) == 0
+    direct = width % LANES == 0 and chips == 4
     swap = [(i, i ^ 1) for i in range(tp_size)]
 
     group_t = group_latent.T
@@ -346,19 +349,31 @@
         )
         return summed.astype(jnp.bfloat16)
 
-    groups = [[chips - 1], list(range(1, chips - 1)), [0]]
-    arrived = []
-    for deltas in groups:
-        sent = project(head_out, upper[0], lower[0], width, deltas, True)
-        arrived.append([lax.ppermute(block, "tp", swap) for block in sent])
-    moved = []
-    for deltas, blocks in zip(groups, arrived):
-        sums = project(head_out, upper[0], lower[0], width, deltas, False, tuple(blocks))
-        for delta, block in zip(deltas, sums):
-            if delta:
-                block = lax.ppermute(block, "tp", [(i, i ^ (2 * delta)) for i in range(tp_size)])
-            moved.append(block.astype(jnp.float32))
-    return sum(moved).astype(jnp.bfloat16)
+    def move(block, delta):
+        return lax.ppermute(block, "tp", [(i, i ^ delta) for i in range(tp_size)])
+
+    def plus(first, second):
+        return (first.astype(jnp.float32) + second.astype(jnp.float32)).astype(jnp.bfloat16)
+
+    run = functools.partial(project, upper=upper[0], lower=lower[0], width=width)
+    far = [move(block, 1) for block in run(head_out, deltas=[3], theirs=True)]
+    near = [move(block, 1) for block in run(head_out, deltas=[1, 2], theirs=True)]
+    far_top, far_low = run(head_out, deltas=[3], theirs=False, arrived=far, parts=2)
+    via_first = move(far_top, 2)
+    via_second = move(far_low, 4)
+    first_top, first_low, second_top, second_low = run(
+        head_out, deltas=[1, 2], theirs=False, arrived=near, parts=2
+    )
+    got_first_top = move(first_top, 2)
+    got_second_low = move(second_low, 4)
+    later, first_low, second_top = lax.optimization_barrier((head_out, first_low, second_top))
+    own = [move(block, 1) for block in run(later, deltas=[0], theirs=True)]
+    got_first_low = move(plus(first_low, via_second), 2)
+    got_second_top = move(plus(second_top, via_first), 4)
+    own_top, own_low = run(later, deltas=[0], theirs=False, arrived=own, parts=2)
+    halves = [(own_top, got_first_top, got_second_top), (own_low, got_first_low, got_second_low)]
+    summed = [sum(block.astype(jnp.float32) for block in half) for half in halves]
+    return jnp.concatenate(summed, 0).astype(jnp.bfloat16)
 
 
 def solution(mesh):

time: 49.5 us -> 47.1 us (0.952)
  waiting for transfers between devices: 15.7 us -> 10.4 us
  starting transfers between devices: 11.1 us -> 14.7 us
  Pallas kernels: 20.6 us -> 19.9 us
    ppermute x7 -> x10, waiting for transfers between devices: 8.22 us -> 2.96 us  [move(): return lax.ppermute(block, 'tp', [(i, i ^ delta) for i in range(tp_size)])]
    ppermute x7 -> x10, starting transfers between devices: 4.91 us -> 8.46 us  [move(): return lax.ppermute(block, 'tp', [(i, i ^ delta) for i in range(tp_size)])]
    pallas_call x1, Pallas kernels: 7.72 us -> 6.93 us  [attend(): pl.pallas_call(functools.partial(attend_kernel, step, base), in_specs=in_...]
    convert_element_type x1 -> x2, other arithmetic: 0.82 us -> 0.06 us  [plus(): (first.astype(jnp.float32) + second.astype(jnp.float32)).astype(jnp.bfloa...]
    concatenate x0 -> x1, other arithmetic: none -> 0.71 us  [layer(): return jnp.concatenate(summed, 0).astype(jnp.bfloat16)]
  transfers between devices with their start and end apart: 11 -> 14, of which waited for: 4 -> 4; matrix products, arithmetic and copies ran while one was open for 0% -> 0% of each run, Pallas kernels for 23% -> 24%
where the time goes in v3:
time: 47.1 us; the launch traced here: 46.9 us
  Pallas kernels  19.9 us (42%)
  starting transfers between devices  14.7 us (31%)
  waiting for transfers between devices  10.4 us (22%)
  other arithmetic  0.9 us (2%)
  between operations  0.82 us (2%)
    ppermute x10, starting transfers between devices, move(): return lax.ppermute(block, 'tp', [(i, i ^ delta) for i in range(tp_size)])  8.46 us
    ppermute x3, waiting for transfers between devices, layer(): arrived.append(lax.ppermute(part, 'ctx', ring))  7.44 us
    pallas_call x1, Pallas kernels, attend(): pl.pallas_call(functools.partial(attend_kernel, step, base), in_specs=in_...  6.93 us
    pallas_call x1, Pallas kernels, front(): pl.pallas_call(functools.partial(front_kernel, weight is not None), in_sp...  6.36 us
    ppermute x3, starting transfers between devices, layer(): arrived.append(lax.ppermute(part, 'ctx', ring))  6.14 us
    pallas_call x6, Pallas kernels, project(): pl.pallas_call(functools.partial(project_kernel, width, deltas, theirs, b...  5.65 us
    ppermute x10, waiting for transfers between devices, move(): return lax.ppermute(block, 'tp', [(i, i ^ delta) for i in range(tp_size)])  2.96 us
  transfers between devices with their start and end apart: 14, of which 4 were waited for; matrix products, arithmetic and copies ran while one was open for 0% of the time, Pallas kernels for 24%

profile of v3, /device:TPU:0, one launch (start us, length us, event | category | flops | bytes accessed | tf_op | source)
XLA Modules:
  0.0 46.9 jit_solution(15603757033802123184)
XLA Ops:
  0.0 0.9 %pack.1 = bf16[368,128]{1,0:T(8,128)(2,1)S(1)} custom-call(bf16[576,128]{1,0:T(8,128)(2,1)} %bitcast.4, bf16[32,576]{1,0:T(8,128)(2,1)} %cache_ref.3), custom_call_target="tpu_custom_call" | custom-call | tf_op jit(solution)/shard_map/pack/pallas_call | solution.py:48
  0.9 5.1 %collective-permute-start.2 = (bf16[368,128]{1,0:T(8,128)(2,1)S(1)}, bf16[368,128]{1,0:T(8,128)(2,1)S(1)}, u32[]{:S(2)}, u32[]{:S(2)}) collective-permute-start(bf16[368,128]{1,0:T(8,128)(2,1)S(1)} %pack.1), channel_id=1, source_target_pairs={{0,24},{8,0},{16,8},{24,16},{1,25},{9,1},{17,9},{25,17},{2,26},{10... | collective-permute-start | bytes 282632 | tf_op jit(solution)/shard_map/ppermute | solution.py:334
  6.1 0.0 collective-permute-start.1
  6.1 1.0 %collective-permute-start = (bf16[368,128]{1,0:T(8,128)(2,1)S(1)}, bf16[368,128]{1,0:T(8,128)(2,1)S(1)}, u32[]{:S(2)}, u32[]{:S(2)}) collective-permute-start(bf16[368,128]{1,0:T(8,128)(2,1)S(1)} %pack.1), channel_id=1, source_target_pairs={{0,8},{8,16},{16,24},{24,0},{1,9},{9,17},{17,25},{25,1},{2,10},{10... | collective-permute-start | bytes 282632 | tf_op jit(solution)/shard_map/ppermute | solution.py:334
  7.1 2.1 %collective-permute-done.2 = bf16[368,128]{1,0:T(8,128)(2,1)S(1)} collective-permute-done((bf16[368,128]{1,0:T(8,128)(2,1)S(1)}, bf16[368,128]{1,0:T(8,128)(2,1)S(1)}, u32[]{:S(2)}, u32[]{:S(2)}) %collective-permute-start.2) | collective-permute-done | bytes 94240 | tf_op jit(solution)/shard_map/ppermute | solution.py:334
  9.2 5.4 %collective-permute-done.1 = bf16[368,128]{1,0:T(8,128)(2,1)S(1)} collective-permute-done((bf16[368,128]{1,0:T(8,128)(2,1)S(1)}, bf16[368,128]{1,0:T(8,128)(2,1)S(1)}, u32[]{:S(2)}, u32[]{:S(2)}) %collective-permute-start.1) | collective-permute-done | bytes 94240 | tf_op jit(solution)/shard_map/ppermute | solution.py:334
  14.5 0.0 collective-permute-done
  14.5 0.1 collective-permute-start.3
  15.3 0.0 copy-start
  15.3 0.0 copy-start.1
  15.3 0.0 copy-start.2
  15.3 0.0 copy-start.3
  15.3 6.4 %front.1 = (bf16[16,128,640]{2,1,0:T(8,128)(2,1)S(1)}, f32[32,512]{1,0:T(8,128)S(1)}, f32[32,512]{1,0:T(8,128)S(1)}, bf16[1024,7168]{1,0:T(8,128)(2,1)S(1)}) custom-call(s32[1]{0:T(128)S(6)} %copy.10.offset_ref, bf16[128,2048]{1,0:T(8,128)(2,1)} %nope_hbm.1, bf16[128,1024]{1,0:T(8,128)(2,1)} %rope_hbm.1, bf16[16,128,512]{2,1,0:T(8,128)(2,1)} %up_hbm.1, ...), custom_call_target="tpu_custom_call" | custom-call | flops 268435456 | bytes 37748736 | tf_op jit(solution)/shard_map/front/pallas_call | solution.py:146
  21.7 0.0 collective-permute-done.3.theirs_ref
  21.7 0.2 copy-done
  21.9 0.0 copy-done.1
  21.9 0.0 copy-done.2
  21.9 0.0 copy-done.3
  21.9 6.9 %attend.1 = (bf16[128,2048]{1,0:T(8,128)(2,1)S(1)}, bf16[1024,7168]{1,0:T(8,128)(2,1)S(1)}) custom-call(s32[4]{0:T(128)S(1)} %copy-done.3, bf16[16,128,640]{2,1,0:T(8,128)(2,1)S(1)} %get-tuple-element.24.q_ref, bf16[3,368,128]{2,1,0:T(8,128)(2,1)S(1)} %pad_maximum_fusion.mine_ref, bf16[3,368,128]{2,1,0:T(8,128)(2,1)S(1)} %collective-permute-done.3.theirs_ref, ...), custom_call_target="tpu_custom_call" | custom-call | flops 3019898880 | bytes 8388608 | tf_op jit(solution)/shard_map/attend/pallas_call | solution.py:266
  28.9 0.8 %project.10 = bf16[128,896]{1,0:T(8,128)(2,1)S(1)} custom-call(bf16[128,2048]{1,0:T(8,128)(2,1)S(1)} %get-tuple-element.34.head_ref, bf16[1024,7168]{1,0:T(8,128)(2,1)S(1)} %get-tuple-element.28.upper_ref, bf16[1024,7168]{1,0:T(8,128)(2,1)S(1)} %get-tuple-element.29.lower_ref), custom_call_target="tpu_custom_call" | custom-call | flops 469762048 | bytes 229376 | tf_op jit(solution)/shard_map/project/pallas_call | solution.py:305
  29.7 0.6 %collective-permute-start.8 = (bf16[128,896]{1,0:T(8,128)(2,1)S(1)}, bf16[128,896]{1,0:T(8,128)(2,1)S(1)}, u32[]{:S(2)}, u32[]{:S(2)}) collective-permute-start(bf16[128,896]{1,0:T(8,128)(2,1)S(1)} %project.10), channel_id=1, source_target_pairs={{0,1},{1,0},{2,3},{3,2},{4,5},{5,4},{6,7},{7,6},{8,9},{9,8},{10,11... | collective-permute-start | bytes 688136 | tf_op jit(solution)/shard_map/ppermute | solution.py:353
  30.2 1.3 %project.6 = (bf16[128,896]{1,0:T(8,128)(2,1)S(1)}, bf16[128,896]{1,0:T(8,128)(2,1)S(1)}) custom-call(bf16[128,2048]{1,0:T(8,128)(2,1)S(1)} %get-tuple-element.34.head_ref, bf16[1024,7168]{1,0:T(8,128)(2,1)S(1)} %get-tuple-element.28.upper_ref, bf16[1024,7168]{1,0:T(8,128)(2,1)S(1)} %get-tuple-element.29.lower_ref), custom_call_target="tpu_custom_call" | custom-call | flops 939524096 | bytes 458752 | tf_op jit(solution)/shard_map/project/pallas_call | solution.py:305
  31.6 0.1 collective-permute-start.4
  31.6 0.5 %collective-permute-start.5 = (bf16[128,896]{1,0:T(8,128)(2,1)S(1)}, bf16[128,896]{1,0:T(8,128)(2,1)S(1)}, u32[]{:S(2)}, u32[]{:S(2)}) collective-permute-start(bf16[128,896]{1,0:T(8,128)(2,1)S(1)} %get-tuple-element.31), channel_id=1, source_target_pairs={{0,1},{1,0},{2,3},{3,2},{4,5},{5,4},{6,7},{7,6},{8,9},{9,8},{10,11... | collective-permute-start | bytes 688136 | tf_op jit(solution)/shard_map/ppermute | solution.py:353
  32.1 0.0 collective-permute-done.8.refs_0_
  32.1 0.8 %project.11 = (bf16[64,896]{1,0:T(8,128)(2,1)S(1)}, bf16[64,896]{1,0:T(8,128)(2,1)S(1)}) custom-call(bf16[128,2048]{1,0:T(8,128)(2,1)S(1)} %get-tuple-element.34.head_ref, bf16[1024,7168]{1,0:T(8,128)(2,1)S(1)} %get-tuple-element.28.upper_ref, bf16[1024,7168]{1,0:T(8,128)(2,1)S(1)} %get-tuple-element.29.lower_ref, ...), custom_call_target="tpu_custom_call" | custom-call | flops 469762048 | bytes 229376 | tf_op jit(solution)/shard_map/project/pallas_call | solution.py:305
  32.9 1.5 %collective-permute-start.9 = (bf16[64,896]{1,0:T(8,128)(2,1)S(1)}, bf16[64,896]{1,0:T(8,128)(2,1)S(1)}, u32[]{:S(2)}, u32[]{:S(2)}) collective-permute-start(bf16[64,896]{1,0:T(8,128)(2,1)S(1)} %get-tuple-element.38), channel_id=1, source_target_pairs={{0,2},{1,3},{2,0},{3,1},{4,6},{5,7},{6,4},{7,5},{8,10},{9,11},{10,... | collective-permute-start | bytes 344072 | tf_op jit(solution)/shard_map/ppermute | solution.py:353
  34.4 1.5 %collective-permute-start.11 = (bf16[64,896]{1,0:T(8,128)(2,1)S(1)}, bf16[64,896]{1,0:T(8,128)(2,1)S(1)}, u32[]{:S(2)}, u32[]{:S(2)}) collective-permute-start(bf16[64,896]{1,0:T(8,128)(2,1)S(1)} %get-tuple-element.41), channel_id=1, source_target_pairs={{0,4},{1,5},{2,6},{3,7},{4,0},{5,1},{6,2},{7,3},{8,12},{9,13},{10,... | collective-permute-start | bytes 344072 | tf_op jit(solution)/shard_map/ppermute | solution.py:353
  35.9 0.0 collective-permute-done.4.refs_0_
  35.9 0.0 collective-permute-done.5.refs_1_
  35.9 1.3 %project.7 = (bf16[64,896]{1,0:T(8,128)(2,1)S(1)}, bf16[64,896]{1,0:T(8,128)(2,1)S(1)}, bf16[64,896]{1,0:T(8,128)(2,1)S(1)}, bf16[64,896]{1,0:T(8,128)(2,1)S(1)}) custom-call(bf16[128,2048]{1,0:T(8,128)(2,1)S(1)} %get-tuple-element.34.head_ref, bf16[1024,7168]{1,0:T(8,128)(2,1)S(1)} %get-tuple-element.28.upper_ref, ...), custom_call_target="tpu_custom_call" | custom-call | flops 939524096 | bytes 458752 | tf_op jit(solution)/shard_map/project/pallas_call | solution.py:305
  37.2 0.6 %collective-permute-start.7 = (bf16[64,896]{1,0:T(8,128)(2,1)S(1)}, bf16[64,896]{1,0:T(8,128)(2,1)S(1)}, u32[]{:S(2)}, u32[]{:S(2)}) collective-permute-start(bf16[64,896]{1,0:T(8,128)(2,1)S(1)} %get-tuple-element.36), channel_id=1, source_target_pairs={{0,2},{1,3},{2,0},{3,1},{4,6},{5,7},{6,4},{7,5},{8,10},{9,11},{10,... | collective-permute-start | bytes 344072 | tf_op jit(solution)/shard_map/ppermute | solution.py:353
  37.9 0.6 %collective-permute-start.13 = (bf16[64,896]{1,0:T(8,128)(2,1)S(1)}, bf16[64,896]{1,0:T(8,128)(2,1)S(1)}, u32[]{:S(2)}, u32[]{:S(2)}) collective-permute-start(bf16[64,896]{1,0:T(8,128)(2,1)S(1)} %get-tuple-element.42), channel_id=1, source_target_pairs={{0,4},{1,5},{2,6},{3,7},{4,0},{5,1},{6,2},{7,3},{8,12},{9,13},{10,... | collective-permute-start | bytes 344072 | tf_op jit(solution)/shard_map/ppermute | solution.py:353
  38.4 0.7 %project.8 = bf16[128,896]{1,0:T(8,128)(2,1)S(1)} custom-call(bf16[128,2048]{1,0:T(8,128)(2,1)S(1)} %get-tuple-element.34.head_ref, bf16[1024,7168]{1,0:T(8,128)(2,1)S(1)} %get-tuple-element.28.upper_ref, bf16[1024,7168]{1,0:T(8,128)(2,1)S(1)} %get-tuple-element.29.lower_ref), custom_call_target="tpu_custom_call" | custom-call | flops 469762048 | bytes 229376 | tf_op jit(solution)/shard_map/project/pallas_call | solution.py:305
  39.2 0.1 collective-permute-start.6
  39.2 0.0 collective-permute-done.11
  39.3 1.5 %collective-permute-start.12 = (bf16[64,896]{1,0:T(8,128)(2,1)S(1)}, bf16[64,896]{1,0:T(8,128)(2,1)S(1)}, u32[]{:S(2)}, u32[]{:S(2)}) collective-permute-start(bf16[64,896]{1,0:T(8,128)(2,1)S(1)} %add_convert_fusion.1), channel_id=1, source_target_pairs={{0,2},{1,3},{2,0},{3,1},{4,6},{5,7},{6,4},{7,5},{8,10},{9,11},{10,... | collective-permute-start | bytes 344072 | tf_op jit(solution)/shard_map/ppermute | solution.py:353
  40.8 0.0 collective-permute-done.9
  40.8 1.6 %collective-permute-start.10 = (bf16[64,896]{1,0:T(8,128)(2,1)S(1)}, bf16[64,896]{1,0:T(8,128)(2,1)S(1)}, u32[]{:S(2)}, u32[]{:S(2)}) collective-permute-start(bf16[64,896]{1,0:T(8,128)(2,1)S(1)} %add_convert_fusion.3), channel_id=1, source_target_pairs={{0,4},{1,5},{2,6},{3,7},{4,0},{5,1},{6,2},{7,3},{8,12},{9,13},{10,... | collective-permute-start | bytes 344072 | tf_op jit(solution)/shard_map/ppermute | solution.py:353
  42.4 0.0 collective-permute-done.6.refs_0_
  42.4 0.7 %project.9 = (bf16[64,896]{1,0:T(8,128)(2,1)S(1)}, bf16[64,896]{1,0:T(8,128)(2,1)S(1)}) custom-call(bf16[128,2048]{1,0:T(8,128)(2,1)S(1)} %get-tuple-element.34.head_ref, bf16[1024,7168]{1,0:T(8,128)(2,1)S(1)} %get-tuple-element.28.upper_ref, bf16[1024,7168]{1,0:T(8,128)(2,1)S(1)} %get-tuple-element.29.lower_ref, ...), custom_call_target="tpu_custom_call" | custom-call | flops 469762048 | bytes 229376 | tf_op jit(solution)/shard_map/project/pallas_call | solution.py:305
  43.2 0.0 collective-permute-done.13
  43.2 1.7 %collective-permute-done.12 = bf16[64,896]{1,0:T(8,128)(2,1)S(1)} collective-permute-done((bf16[64,896]{1,0:T(8,128)(2,1)S(1)}, bf16[64,896]{1,0:T(8,128)(2,1)S(1)}, u32[]{:S(2)}, u32[]{:S(2)}) %collective-permute-start.12) | collective-permute-done | bytes 114720 | tf_op jit(solution)/shard_map/ppermute | solution.py:353
  45.0 0.0 collective-permute-done.7
  45.0 1.2 %collective-permute-done.10 = bf16[64,896]{1,0:T(8,128)(2,1)S(1)} collective-permute-done((bf16[64,896]{1,0:T(8,128)(2,1)S(1)}, bf16[64,896]{1,0:T(8,128)(2,1)S(1)}, u32[]{:S(2)}, u32[]{:S(2)}) %collective-permute-start.10) | collective-permute-done | bytes 114720 | tf_op jit(solution)/shard_map/ppermute | solution.py:353
  46.2 0.7 %pad_maximum_fusion.1 = bf16[128,896]{1,0:T(8,128)(2,1)} fusion(bf16[64,896]{1,0:T(8,128)(2,1)S(1)} %add_convert_fusion, bf16[64,896]{1,0:T(8,128)(2,1)S(1)} %add_convert_fusion.2), kind=kLoop, calls=%fused_computation.1 | loop fusion | flops 458752 | bytes 458752 | tf_op jit(solution)/shard_map/concatenate | solution.py:376
  (5 shorter events, 0.2 us)
Async XLA Ops:
  0.9 8.2 %collective-permute-start.2 = (bf16[368,128]{1,0:T(8,128)(2,1)S(1)}, bf16[368,128]{1,0:T(8,128)(2,1)S(1)}, u32[]{:S(2)}, u32[]{:S(2)}) collective-permute-start(bf16[368,128]{1,0:T(8,128)(2,1)S(1)} %pack.1), channel_id=1, source_target_pairs={{0,24},{8,0},{16,8},{24,16},{1,25},{9,1},{17,9},{25,17},{2,26},{10... | collective-permute-start | bytes 282632 | tf_op jit(solution)/shard_map/ppermute | solution.py:334
  6.1 8.4 %collective-permute-start.1 = (bf16[368,128]{1,0:T(8,128)(2,1)S(1)}, bf16[368,128]{1,0:T(8,128)(2,1)S(1)}, u32[]{:S(2)}, u32[]{:S(2)}) collective-permute-start(bf16[368,128]{1,0:T(8,128)(2,1)S(1)} %pack.1), channel_id=1, source_target_pairs={{0,16},{8,24},{16,0},{24,8},{1,17},{9,25},{17,1},{25,9},{2,18},{10... | collective-permute-start | bytes 282632 | tf_op jit(solution)/shard_map/ppermute | solution.py:334
  6.1 8.4 %collective-permute-start = (bf16[368,128]{1,0:T(8,128)(2,1)S(1)}, bf16[368,128]{1,0:T(8,128)(2,1)S(1)}, u32[]{:S(2)}, u32[]{:S(2)}) collective-permute-start(bf16[368,128]{1,0:T(8,128)(2,1)S(1)} %pack.1), channel_id=1, source_target_pairs={{0,8},{8,16},{16,24},{24,0},{1,9},{9,17},{17,25},{25,1},{2,10},{10... | collective-permute-start | bytes 282632 | tf_op jit(solution)/shard_map/ppermute | solution.py:334
  14.5 7.1 %collective-permute-start.3 = (bf16[3,368,128]{2,1,0:T(8,128)(2,1)S(1)}, bf16[3,368,128]{2,1,0:T(8,128)(2,1)S(1)}, u32[]{:S(2)}, u32[]{:S(2)}) collective-permute-start(bf16[3,368,128]{2,1,0:T(8,128)(2,1)S(1)} %pad_maximum_fusion.mine_ref), channel_id=1, source_target_pairs={{0,1},{1,0},{2,3},{3,2},{4,5},{5,4},{6,7},{7,6},{8,9},{9,8},{10,11... | collective-permute-start | bytes 847880 | tf_op jit(solution)/shard_map/ppermute | solution.py:336
  15.3 6.7 %copy-start = (bf16[16,512,128]{2,1,0:T(8,128)(2,1)S(1)}, bf16[16,512,128]{2,1,0:T(8,128)(2,1)}, u32[]{:S(2)}) copy-start(bf16[16,512,128]{2,1,0:T(8,128)(2,1)} %refs_2_.1) | copy-start | bytes 6291460
  15.3 6.7 %copy-start.1 = (bf16[128,576]{0,1:T(8,128)(2,1)S(1)}, bf16[128,576]{0,1:T(8,128)(2,1)}, u32[]{:S(2)}) copy-start(bf16[128,576]{0,1:T(8,128)(2,1)} %param.12) | copy-start | bytes 442372
  15.3 6.6 %copy-start.2 = (bf16[32,576]{1,0:T(8,128)(2,1)S(1)}, bf16[32,576]{1,0:T(8,128)(2,1)}, u32[]{:S(2)}) copy-start(bf16[32,576]{1,0:T(8,128)(2,1)} %cache_ref.3) | copy-start | bytes 110596
  15.3 6.6 %copy-start.3 = (s32[4]{0:T(128)S(1)}, s32[4]{0:T(128)}, u32[]{:S(2)}) copy-start(s32[4]{0:T(128)} %counts_ref.1) | copy-start | bytes 52
  29.7 2.5 %collective-permute-start.8 = (bf16[128,896]{1,0:T(8,128)(2,1)S(1)}, bf16[128,896]{1,0:T(8,128)(2,1)S(1)}, u32[]{:S(2)}, u32[]{:S(2)}) collective-permute-start(bf16[128,896]{1,0:T(8,128)(2,1)S(1)} %project.10), channel_id=1, source_target_pairs={{0,1},{1,0},{2,3},{3,2},{4,5},{5,4},{6,7},{7,6},{8,9},{9,8},{10,11... | collective-permute-start | bytes 688136 | tf_op jit(solution)/shard_map/ppermute | solution.py:353
  31.6 4.4 %collective-permute-start.4 = (bf16[128,896]{1,0:T(8,128)(2,1)S(1)}, bf16[128,896]{1,0:T(8,128)(2,1)S(1)}, u32[]{:S(2)}, u32[]{:S(2)}) collective-permute-start(bf16[128,896]{1,0:T(8,128)(2,1)S(1)} %get-tuple-element.30), channel_id=1, source_target_pairs={{0,1},{1,0},{2,3},{3,2},{4,5},{5,4},{6,7},{7,6},{8,9},{9,8},{10,11... | collective-permute-start | bytes 688136 | tf_op jit(solution)/shard_map/ppermute | solution.py:353
  31.6 4.3 %collective-permute-start.5 = (bf16[128,896]{1,0:T(8,128)(2,1)S(1)}, bf16[128,896]{1,0:T(8,128)(2,1)S(1)}, u32[]{:S(2)}, u32[]{:S(2)}) collective-permute-start(bf16[128,896]{1,0:T(8,128)(2,1)S(1)} %get-tuple-element.31), channel_id=1, source_target_pairs={{0,1},{1,0},{2,3},{3,2},{4,5},{5,4},{6,7},{7,6},{8,9},{9,8},{10,11... | collective-permute-start | bytes 688136 | tf_op jit(solution)/shard_map/ppermute | solution.py:353
  32.9 7.9 %collective-permute-start.9 = (bf16[64,896]{1,0:T(8,128)(2,1)S(1)}, bf16[64,896]{1,0:T(8,128)(2,1)S(1)}, u32[]{:S(2)}, u32[]{:S(2)}) collective-permute-start(bf16[64,896]{1,0:T(8,128)(2,1)S(1)} %get-tuple-element.38), channel_id=1, source_target_pairs={{0,2},{1,3},{2,0},{3,1},{4,6},{5,7},{6,4},{7,5},{8,10},{9,11},{10,... | collective-permute-start | bytes 344072 | tf_op jit(solution)/shard_map/ppermute | solution.py:353
  34.4 4.9 %collective-permute-start.11 = (bf16[64,896]{1,0:T(8,128)(2,1)S(1)}, bf16[64,896]{1,0:T(8,128)(2,1)S(1)}, u32[]{:S(2)}, u32[]{:S(2)}) collective-permute-start(bf16[64,896]{1,0:T(8,128)(2,1)S(1)} %get-tuple-element.41), channel_id=1, source_target_pairs={{0,4},{1,5},{2,6},{3,7},{4,0},{5,1},{6,2},{7,3},{8,12},{9,13},{10,... | collective-permute-start | bytes 344072 | tf_op jit(solution)/shard_map/ppermute | solution.py:353
  37.2 7.7 %collective-permute-start.7 = (bf16[64,896]{1,0:T(8,128)(2,1)S(1)}, bf16[64,896]{1,0:T(8,128)(2,1)S(1)}, u32[]{:S(2)}, u32[]{:S(2)}) collective-permute-start(bf16[64,896]{1,0:T(8,128)(2,1)S(1)} %get-tuple-element.36), channel_id=1, source_target_pairs={{0,2},{1,3},{2,0},{3,1},{4,6},{5,7},{6,4},{7,5},{8,10},{9,11},{10,... | collective-permute-start | bytes 344072 | tf_op jit(solution)/shard_map/ppermute | solution.py:353
  37.9 5.3 %collective-permute-start.13 = (bf16[64,896]{1,0:T(8,128)(2,1)S(1)}, bf16[64,896]{1,0:T(8,128)(2,1)S(1)}, u32[]{:S(2)}, u32[]{:S(2)}) collective-permute-start(bf16[64,896]{1,0:T(8,128)(2,1)S(1)} %get-tuple-element.42), channel_id=1, source_target_pairs={{0,4},{1,5},{2,6},{3,7},{4,0},{5,1},{6,2},{7,3},{8,12},{9,13},{10,... | collective-permute-start | bytes 344072 | tf_op jit(solution)/shard_map/ppermute | solution.py:353
  39.2 3.3 %collective-permute-start.6 = (bf16[128,896]{1,0:T(8,128)(2,1)S(1)}, bf16[128,896]{1,0:T(8,128)(2,1)S(1)}, u32[]{:S(2)}, u32[]{:S(2)}) collective-permute-start(bf16[128,896]{1,0:T(8,128)(2,1)S(1)} %project.8), channel_id=1, source_target_pairs={{0,1},{1,0},{2,3},{3,2},{4,5},{5,4},{6,7},{7,6},{8,9},{9,8},{10,11... | collective-permute-start | bytes 688136 | tf_op jit(solution)/shard_map/ppermute | solution.py:353
  39.3 5.6 %collective-permute-start.12 = (bf16[64,896]{1,0:T(8,128)(2,1)S(1)}, bf16[64,896]{1,0:T(8,128)(2,1)S(1)}, u32[]{:S(2)}, u32[]{:S(2)}) collective-permute-start(bf16[64,896]{1,0:T(8,128)(2,1)S(1)} %add_convert_fusion.1), channel_id=1, source_target_pairs={{0,2},{1,3},{2,0},{3,1},{4,6},{5,7},{6,4},{7,5},{8,10},{9,11},{10,... | collective-permute-start | bytes 344072 | tf_op jit(solution)/shard_map/ppermute | solution.py:353
  40.8 5.3 %collective-permute-start.10 = (bf16[64,896]{1,0:T(8,128)(2,1)S(1)}, bf16[64,896]{1,0:T(8,128)(2,1)S(1)}, u32[]{:S(2)}, u32[]{:S(2)}) collective-permute-start(bf16[64,896]{1,0:T(8,128)(2,1)S(1)} %add_convert_fusion.3), channel_id=1, source_target_pairs={{0,4},{1,5},{2,6},{3,7},{4,0},{5,1},{6,2},{7,3},{8,12},{9,13},{10,... | collective-permute-start | bytes 344072 | tf_op jit(solution)/shard_map/ppermute | solution.py:353

commit v4 on v3

--- a/solution.py
+++ b/solution.py
@@ -20,6 +20,7 @@
 HIDDEN = -1e30
 LOG2E = 1.4426950408889634
 STREAMS = 8
+SCALE = LOG2E / math.sqrt(NOPE + ROPE)
 MIB = 1 << 20
 
 
@@ -109,12 +110,12 @@
             latent = jnp.dot(
                 nope, up_ref[group * pair + head], preferred_element_type=jnp.float32
             )
-            out_ref[group * pair + head, :, :LATENT] = latent.astype(jnp.bfloat16)
+            out_ref[group * pair + head, :, :LATENT] = (latent * SCALE).astype(jnp.bfloat16)
             raw = ropes[:, head * ROPE : (head + 1) * ROPE]
             swapped = jnp.concatenate([raw[:, HALF:], raw[:, :HALF]], 1)
             turned = raw * turn_ref[:, :ROPE] + swapped * turn_ref[:, ROPE:]
             pad = jnp.zeros((tokens, WIDE - ENTRIES), jnp.float32)
-            filled = jnp.concatenate([turned, pad], 1)
+            filled = jnp.concatenate([turned * SCALE, pad], 1)
             out_ref[group * pair + head, :, LATENT:] = filled.astype(jnp.bfloat16)
 
     if fetch:
@@ -214,15 +215,21 @@
     keys_ref[:, size * tokens :] = cached_ref[...].T.astype(jnp.bfloat16)
 
     width = q_ref.shape[2]
-    scale = LOG2E / math.sqrt(NOPE + ROPE)
 
     @pl.loop(0, q_ref.shape[0] // step)
     def _(group):
         queries = q_ref[pl.ds(group * step, step)].reshape(step * tokens, width)
-        scores = jnp.dot(queries, keys_ref[...], preferred_element_type=jnp.float32)
+        tail = size * tokens
+        scores = jnp.concatenate(
+            [
+                jnp.dot(queries, keys_ref[:, :tail], preferred_element_type=jnp.float32),
+                jnp.dot(queries, keys_ref[:, tail:], preferred_element_type=jnp.float32),
+            ],
+            1,
+        )
         scores = scores.reshape(step, tokens, -1) + bias_ref[...][None]
         peak = jnp.max(scores, axis=2, keepdims=True)
-        expos = jnp.exp2((scores - peak) * scale)
+        expos = jnp.exp2(scores - peak)
         total = jnp.sum(expos, axis=2, keepdims=True)
         weights = expos.astype(jnp.bfloat16).reshape(step * tokens, -1)
         mixed = lax.dot_general(

time: 47.1 us -> 47.1 us (level)
  no operation moved by 1% of the time
where the time goes in v4:
time: 47.1 us; the launch traced here: 46.9 us
  Pallas kernels  19.9 us (42%)
  starting transfers between devices  14.7 us (31%)
  waiting for transfers between devices  10.4 us (22%)
  other arithmetic  0.9 us (2%)
  between operations  0.82 us (2%)
    ppermute x10, starting transfers between devices, move(): return lax.ppermute(block, 'tp', [(i, i ^ delta) for i in range(tp_size)])  8.45 us
    ppermute x3, waiting for transfers between devices, layer(): arrived.append(lax.ppermute(part, 'ctx', ring))  7.44 us
    pallas_call x1, Pallas kernels, attend(): pl.pallas_call(functools.partial(attend_kernel, step, base), in_specs=in_...  6.93 us
    pallas_call x1, Pallas kernels, front(): pl.pallas_call(functools.partial(front_kernel, weight is not None), in_sp...  6.36 us
    ppermute x3, starting transfers between devices, layer(): arrived.append(lax.ppermute(part, 'ctx', ring))  6.14 us
    pallas_call x6, Pallas kernels, project(): pl.pallas_call(functools.partial(project_kernel, width, deltas, theirs, b...  5.65 us
    ppermute x10, waiting for transfers between devices, move(): return lax.ppermute(block, 'tp', [(i, i ^ delta) for i in range(tp_size)])  3 us
  transfers between devices with their start and end apart: 14, of which 4 were waited for; matrix products, arithmetic and copies ran while one was open for 0% of the time, Pallas kernels for 24%

profile of v4, /device:TPU:0, one launch (start us, length us, event | category | flops | bytes accessed | tf_op | source)
XLA Modules:
  0.0 46.9 jit_solution(3340435227314584706)
XLA Ops:
  0.0 0.9 %pack.1 = bf16[368,128]{1,0:T(8,128)(2,1)S(1)} custom-call(bf16[576,128]{1,0:T(8,128)(2,1)} %bitcast.4, bf16[32,576]{1,0:T(8,128)(2,1)} %cache_ref.3), custom_call_target="tpu_custom_call" | custom-call | tf_op jit(solution)/shard_map/pack/pallas_call | solution.py:49
  0.9 5.1 %collective-permute-start.2 = (bf16[368,128]{1,0:T(8,128)(2,1)S(1)}, bf16[368,128]{1,0:T(8,128)(2,1)S(1)}, u32[]{:S(2)}, u32[]{:S(2)}) collective-permute-start(bf16[368,128]{1,0:T(8,128)(2,1)S(1)} %pack.1), channel_id=1, source_target_pairs={{0,24},{8,0},{16,8},{24,16},{1,25},{9,1},{17,9},{25,17},{2,26},{10... | collective-permute-start | bytes 282632 | tf_op jit(solution)/shard_map/ppermute | solution.py:341
  6.1 0.0 collective-permute-start.1
  6.1 1.0 %collective-permute-start = (bf16[368,128]{1,0:T(8,128)(2,1)S(1)}, bf16[368,128]{1,0:T(8,128)(2,1)S(1)}, u32[]{:S(2)}, u32[]{:S(2)}) collective-permute-start(bf16[368,128]{1,0:T(8,128)(2,1)S(1)} %pack.1), channel_id=1, source_target_pairs={{0,8},{8,16},{16,24},{24,0},{1,9},{9,17},{17,25},{25,1},{2,10},{10... | collective-permute-start | bytes 282632 | tf_op jit(solution)/shard_map/ppermute | solution.py:341
  7.1 2.1 %collective-permute-done.2 = bf16[368,128]{1,0:T(8,128)(2,1)S(1)} collective-permute-done((bf16[368,128]{1,0:T(8,128)(2,1)S(1)}, bf16[368,128]{1,0:T(8,128)(2,1)S(1)}, u32[]{:S(2)}, u32[]{:S(2)}) %collective-permute-start.2) | collective-permute-done | bytes 94240 | tf_op jit(solution)/shard_map/ppermute | solution.py:341
  9.2 5.4 %collective-permute-done.1 = bf16[368,128]{1,0:T(8,128)(2,1)S(1)} collective-permute-done((bf16[368,128]{1,0:T(8,128)(2,1)S(1)}, bf16[368,128]{1,0:T(8,128)(2,1)S(1)}, u32[]{:S(2)}, u32[]{:S(2)}) %collective-permute-start.1) | collective-permute-done | bytes 94240 | tf_op jit(solution)/shard_map/ppermute | solution.py:341
  14.5 0.0 collective-permute-done
  14.5 0.1 collective-permute-start.3
  15.3 0.0 copy-start
  15.3 0.0 copy-start.1
  15.3 0.0 copy-start.2
  15.3 0.0 copy-start.3
  15.3 6.4 %front.1 = (bf16[16,128,640]{2,1,0:T(8,128)(2,1)S(1)}, f32[32,512]{1,0:T(8,128)S(1)}, f32[32,512]{1,0:T(8,128)S(1)}, bf16[1024,7168]{1,0:T(8,128)(2,1)S(1)}) custom-call(s32[1]{0:T(128)S(6)} %copy.10.offset_ref, bf16[128,2048]{1,0:T(8,128)(2,1)} %nope_hbm.1, bf16[128,1024]{1,0:T(8,128)(2,1)} %rope_hbm.1, bf16[16,128,512]{2,1,0:T(8,128)(2,1)} %up_hbm.1, ...), custom_call_target="tpu_custom_call" | custom-call | flops 268435456 | bytes 37748736 | tf_op jit(solution)/shard_map/front/pallas_call | solution.py:147
  21.7 0.0 collective-permute-done.3.theirs_ref
  21.7 0.2 copy-done
  21.9 0.0 copy-done.1
  21.9 0.0 copy-done.2
  21.9 0.0 copy-done.3
  21.9 6.9 %attend.1 = (bf16[128,2048]{1,0:T(8,128)(2,1)S(1)}, bf16[1024,7168]{1,0:T(8,128)(2,1)S(1)}) custom-call(s32[4]{0:T(128)S(1)} %copy-done.3, bf16[16,128,640]{2,1,0:T(8,128)(2,1)S(1)} %get-tuple-element.24.q_ref, bf16[3,368,128]{2,1,0:T(8,128)(2,1)S(1)} %pad_maximum_fusion.mine_ref, bf16[3,368,128]{2,1,0:T(8,128)(2,1)S(1)} %collective-permute-done.3.theirs_ref, ...), custom_call_target="tpu_custom_call" | custom-call | flops 3019898880 | bytes 8388608 | tf_op jit(solution)/shard_map/attend/pallas_call | solution.py:273
  28.9 0.8 %project.10 = bf16[128,896]{1,0:T(8,128)(2,1)S(1)} custom-call(bf16[128,2048]{1,0:T(8,128)(2,1)S(1)} %get-tuple-element.34.head_ref, bf16[1024,7168]{1,0:T(8,128)(2,1)S(1)} %get-tuple-element.28.upper_ref, bf16[1024,7168]{1,0:T(8,128)(2,1)S(1)} %get-tuple-element.29.lower_ref), custom_call_target="tpu_custom_call" | custom-call | flops 469762048 | bytes 229376 | tf_op jit(solution)/shard_map/project/pallas_call | solution.py:312
  29.7 0.6 %collective-permute-start.8 = (bf16[128,896]{1,0:T(8,128)(2,1)S(1)}, bf16[128,896]{1,0:T(8,128)(2,1)S(1)}, u32[]{:S(2)}, u32[]{:S(2)}) collective-permute-start(bf16[128,896]{1,0:T(8,128)(2,1)S(1)} %project.10), channel_id=1, source_target_pairs={{0,1},{1,0},{2,3},{3,2},{4,5},{5,4},{6,7},{7,6},{8,9},{9,8},{10,11... | collective-permute-start | bytes 688136 | tf_op jit(solution)/shard_map/ppermute | solution.py:360
  30.2 1.3 %project.6 = (bf16[128,896]{1,0:T(8,128)(2,1)S(1)}, bf16[128,896]{1,0:T(8,128)(2,1)S(1)}) custom-call(bf16[128,2048]{1,0:T(8,128)(2,1)S(1)} %get-tuple-element.34.head_ref, bf16[1024,7168]{1,0:T(8,128)(2,1)S(1)} %get-tuple-element.28.upper_ref, bf16[1024,7168]{1,0:T(8,128)(2,1)S(1)} %get-tuple-element.29.lower_ref), custom_call_target="tpu_custom_call" | custom-call | flops 939524096 | bytes 458752 | tf_op jit(solution)/shard_map/project/pallas_call | solution.py:312
  31.6 0.1 collective-permute-start.4
  31.6 0.5 %collective-permute-start.5 = (bf16[128,896]{1,0:T(8,128)(2,1)S(1)}, bf16[128,896]{1,0:T(8,128)(2,1)S(1)}, u32[]{:S(2)}, u32[]{:S(2)}) collective-permute-start(bf16[128,896]{1,0:T(8,128)(2,1)S(1)} %get-tuple-element.31), channel_id=1, source_target_pairs={{0,1},{1,0},{2,3},{3,2},{4,5},{5,4},{6,7},{7,6},{8,9},{9,8},{10,11... | collective-permute-start | bytes 688136 | tf_op jit(solution)/shard_map/ppermute | solution.py:360
  32.1 0.0 collective-permute-done.8.refs_0_
  32.1 0.8 %project.11 = (bf16[64,896]{1,0:T(8,128)(2,1)S(1)}, bf16[64,896]{1,0:T(8,128)(2,1)S(1)}) custom-call(bf16[128,2048]{1,0:T(8,128)(2,1)S(1)} %get-tuple-element.34.head_ref, bf16[1024,7168]{1,0:T(8,128)(2,1)S(1)} %get-tuple-element.28.upper_ref, bf16[1024,7168]{1,0:T(8,128)(2,1)S(1)} %get-tuple-element.29.lower_ref, ...), custom_call_target="tpu_custom_call" | custom-call | flops 469762048 | bytes 229376 | tf_op jit(solution)/shard_map/project/pallas_call | solution.py:312
  32.9 1.5 %collective-permute-start.9 = (bf16[64,896]{1,0:T(8,128)(2,1)S(1)}, bf16[64,896]{1,0:T(8,128)(2,1)S(1)}, u32[]{:S(2)}, u32[]{:S(2)}) collective-permute-start(bf16[64,896]{1,0:T(8,128)(2,1)S(1)} %get-tuple-element.38), channel_id=1, source_target_pairs={{0,2},{1,3},{2,0},{3,1},{4,6},{5,7},{6,4},{7,5},{8,10},{9,11},{10,... | collective-permute-start | bytes 344072 | tf_op jit(solution)/shard_map/ppermute | solution.py:360
  34.4 1.5 %collective-permute-start.11 = (bf16[64,896]{1,0:T(8,128)(2,1)S(1)}, bf16[64,896]{1,0:T(8,128)(2,1)S(1)}, u32[]{:S(2)}, u32[]{:S(2)}) collective-permute-start(bf16[64,896]{1,0:T(8,128)(2,1)S(1)} %get-tuple-element.41), channel_id=1, source_target_pairs={{0,4},{1,5},{2,6},{3,7},{4,0},{5,1},{6,2},{7,3},{8,12},{9,13},{10,... | collective-permute-start | bytes 344072 | tf_op jit(solution)/shard_map/ppermute | solution.py:360
  35.9 0.0 collective-permute-done.4.refs_0_
  35.9 0.0 collective-permute-done.5.refs_1_
  35.9 1.3 %project.7 = (bf16[64,896]{1,0:T(8,128)(2,1)S(1)}, bf16[64,896]{1,0:T(8,128)(2,1)S(1)}, bf16[64,896]{1,0:T(8,128)(2,1)S(1)}, bf16[64,896]{1,0:T(8,128)(2,1)S(1)}) custom-call(bf16[128,2048]{1,0:T(8,128)(2,1)S(1)} %get-tuple-element.34.head_ref, bf16[1024,7168]{1,0:T(8,128)(2,1)S(1)} %get-tuple-element.28.upper_ref, ...), custom_call_target="tpu_custom_call" | custom-call | flops 939524096 | bytes 458752 | tf_op jit(solution)/shard_map/project/pallas_call | solution.py:312
  37.2 0.6 %collective-permute-start.7 = (bf16[64,896]{1,0:T(8,128)(2,1)S(1)}, bf16[64,896]{1,0:T(8,128)(2,1)S(1)}, u32[]{:S(2)}, u32[]{:S(2)}) collective-permute-start(bf16[64,896]{1,0:T(8,128)(2,1)S(1)} %get-tuple-element.36), channel_id=1, source_target_pairs={{0,2},{1,3},{2,0},{3,1},{4,6},{5,7},{6,4},{7,5},{8,10},{9,11},{10,... | collective-permute-start | bytes 344072 | tf_op jit(solution)/shard_map/ppermute | solution.py:360
  37.9 0.6 %collective-permute-start.13 = (bf16[64,896]{1,0:T(8,128)(2,1)S(1)}, bf16[64,896]{1,0:T(8,128)(2,1)S(1)}, u32[]{:S(2)}, u32[]{:S(2)}) collective-permute-start(bf16[64,896]{1,0:T(8,128)(2,1)S(1)} %get-tuple-element.42), channel_id=1, source_target_pairs={{0,4},{1,5},{2,6},{3,7},{4,0},{5,1},{6,2},{7,3},{8,12},{9,13},{10,... | collective-permute-start | bytes 344072 | tf_op jit(solution)/shard_map/ppermute | solution.py:360
  38.4 0.7 %project.8 = bf16[128,896]{1,0:T(8,128)(2,1)S(1)} custom-call(bf16[128,2048]{1,0:T(8,128)(2,1)S(1)} %get-tuple-element.34.head_ref, bf16[1024,7168]{1,0:T(8,128)(2,1)S(1)} %get-tuple-element.28.upper_ref, bf16[1024,7168]{1,0:T(8,128)(2,1)S(1)} %get-tuple-element.29.lower_ref), custom_call_target="tpu_custom_call" | custom-call | flops 469762048 | bytes 229376 | tf_op jit(solution)/shard_map/project/pallas_call | solution.py:312
  39.2 0.1 collective-permute-start.6
  39.2 0.0 collective-permute-done.11
  39.3 1.5 %collective-permute-start.12 = (bf16[64,896]{1,0:T(8,128)(2,1)S(1)}, bf16[64,896]{1,0:T(8,128)(2,1)S(1)}, u32[]{:S(2)}, u32[]{:S(2)}) collective-permute-start(bf16[64,896]{1,0:T(8,128)(2,1)S(1)} %add_convert_fusion.1), channel_id=1, source_target_pairs={{0,2},{1,3},{2,0},{3,1},{4,6},{5,7},{6,4},{7,5},{8,10},{9,11},{10,... | collective-permute-start | bytes 344072 | tf_op jit(solution)/shard_map/ppermute | solution.py:360
  40.8 0.0 collective-permute-done.9
  40.9 1.6 %collective-permute-start.10 = (bf16[64,896]{1,0:T(8,128)(2,1)S(1)}, bf16[64,896]{1,0:T(8,128)(2,1)S(1)}, u32[]{:S(2)}, u32[]{:S(2)}) collective-permute-start(bf16[64,896]{1,0:T(8,128)(2,1)S(1)} %add_convert_fusion.3), channel_id=1, source_target_pairs={{0,4},{1,5},{2,6},{3,7},{4,0},{5,1},{6,2},{7,3},{8,12},{9,13},{10,... | collective-permute-start | bytes 344072 | tf_op jit(solution)/shard_map/ppermute | solution.py:360
  42.4 0.0 collective-permute-done.6.refs_0_
  42.4 0.7 %project.9 = (bf16[64,896]{1,0:T(8,128)(2,1)S(1)}, bf16[64,896]{1,0:T(8,128)(2,1)S(1)}) custom-call(bf16[128,2048]{1,0:T(8,128)(2,1)S(1)} %get-tuple-element.34.head_ref, bf16[1024,7168]{1,0:T(8,128)(2,1)S(1)} %get-tuple-element.28.upper_ref, bf16[1024,7168]{1,0:T(8,128)(2,1)S(1)} %get-tuple-element.29.lower_ref, ...), custom_call_target="tpu_custom_call" | custom-call | flops 469762048 | bytes 229376 | tf_op jit(solution)/shard_map/project/pallas_call | solution.py:312
  43.2 0.0 collective-permute-done.13
  43.2 1.7 %collective-permute-done.12 = bf16[64,896]{1,0:T(8,128)(2,1)S(1)} collective-permute-done((bf16[64,896]{1,0:T(8,128)(2,1)S(1)}, bf16[64,896]{1,0:T(8,128)(2,1)S(1)}, u32[]{:S(2)}, u32[]{:S(2)}) %collective-permute-start.12) | collective-permute-done | bytes 114720 | tf_op jit(solution)/shard_map/ppermute | solution.py:360
  44.9 0.0 collective-permute-done.7
  45.0 1.2 %collective-permute-done.10 = bf16[64,896]{1,0:T(8,128)(2,1)S(1)} collective-permute-done((bf16[64,896]{1,0:T(8,128)(2,1)S(1)}, bf16[64,896]{1,0:T(8,128)(2,1)S(1)}, u32[]{:S(2)}, u32[]{:S(2)}) %collective-permute-start.10) | collective-permute-done | bytes 114720 | tf_op jit(solution)/shard_map/ppermute | solution.py:360
  46.2 0.7 %pad_maximum_fusion.1 = bf16[128,896]{1,0:T(8,128)(2,1)} fusion(bf16[64,896]{1,0:T(8,128)(2,1)S(1)} %add_convert_fusion, bf16[64,896]{1,0:T(8,128)(2,1)S(1)} %add_convert_fusion.2), kind=kLoop, calls=%fused_computation.1 | loop fusion | flops 458752 | bytes 458752 | tf_op jit(solution)/shard_map/concatenate | solution.py:383
  (5 shorter events, 0.2 us)
Async XLA Ops:
  0.9 8.2 %collective-permute-start.2 = (bf16[368,128]{1,0:T(8,128)(2,1)S(1)}, bf16[368,128]{1,0:T(8,128)(2,1)S(1)}, u32[]{:S(2)}, u32[]{:S(2)}) collective-permute-start(bf16[368,128]{1,0:T(8,128)(2,1)S(1)} %pack.1), channel_id=1, source_target_pairs={{0,24},{8,0},{16,8},{24,16},{1,25},{9,1},{17,9},{25,17},{2,26},{10... | collective-permute-start | bytes 282632 | tf_op jit(solution)/shard_map/ppermute | solution.py:341
  6.1 8.4 %collective-permute-start.1 = (bf16[368,128]{1,0:T(8,128)(2,1)S(1)}, bf16[368,128]{1,0:T(8,128)(2,1)S(1)}, u32[]{:S(2)}, u32[]{:S(2)}) collective-permute-start(bf16[368,128]{1,0:T(8,128)(2,1)S(1)} %pack.1), channel_id=1, source_target_pairs={{0,16},{8,24},{16,0},{24,8},{1,17},{9,25},{17,1},{25,9},{2,18},{10... | collective-permute-start | bytes 282632 | tf_op jit(solution)/shard_map/ppermute | solution.py:341
  6.1 8.4 %collective-permute-start = (bf16[368,128]{1,0:T(8,128)(2,1)S(1)}, bf16[368,128]{1,0:T(8,128)(2,1)S(1)}, u32[]{:S(2)}, u32[]{:S(2)}) collective-permute-start(bf16[368,128]{1,0:T(8,128)(2,1)S(1)} %pack.1), channel_id=1, source_target_pairs={{0,8},{8,16},{16,24},{24,0},{1,9},{9,17},{17,25},{25,1},{2,10},{10... | collective-permute-start | bytes 282632 | tf_op jit(solution)/shard_map/ppermute | solution.py:341
  14.5 7.1 %collective-permute-start.3 = (bf16[3,368,128]{2,1,0:T(8,128)(2,1)S(1)}, bf16[3,368,128]{2,1,0:T(8,128)(2,1)S(1)}, u32[]{:S(2)}, u32[]{:S(2)}) collective-permute-start(bf16[3,368,128]{2,1,0:T(8,128)(2,1)S(1)} %pad_maximum_fusion.mine_ref), channel_id=1, source_target_pairs={{0,1},{1,0},{2,3},{3,2},{4,5},{5,4},{6,7},{7,6},{8,9},{9,8},{10,11... | collective-permute-start | bytes 847880 | tf_op jit(solution)/shard_map/ppermute | solution.py:343
  15.3 6.7 %copy-start = (bf16[16,512,128]{2,1,0:T(8,128)(2,1)S(1)}, bf16[16,512,128]{2,1,0:T(8,128)(2,1)}, u32[]{:S(2)}) copy-start(bf16[16,512,128]{2,1,0:T(8,128)(2,1)} %refs_2_.1) | copy-start | bytes 6291460
  15.3 6.7 %copy-start.1 = (bf16[128,576]{0,1:T(8,128)(2,1)S(1)}, bf16[128,576]{0,1:T(8,128)(2,1)}, u32[]{:S(2)}) copy-start(bf16[128,576]{0,1:T(8,128)(2,1)} %param.12) | copy-start | bytes 442372
  15.3 6.6 %copy-start.2 = (bf16[32,576]{1,0:T(8,128)(2,1)S(1)}, bf16[32,576]{1,0:T(8,128)(2,1)}, u32[]{:S(2)}) copy-start(bf16[32,576]{1,0:T(8,128)(2,1)} %cache_ref.3) | copy-start | bytes 110596
  15.3 6.6 %copy-start.3 = (s32[4]{0:T(128)S(1)}, s32[4]{0:T(128)}, u32[]{:S(2)}) copy-start(s32[4]{0:T(128)} %counts_ref.1) | copy-start | bytes 52
  29.7 2.5 %collective-permute-start.8 = (bf16[128,896]{1,0:T(8,128)(2,1)S(1)}, bf16[128,896]{1,0:T(8,128)(2,1)S(1)}, u32[]{:S(2)}, u32[]{:S(2)}) collective-permute-start(bf16[128,896]{1,0:T(8,128)(2,1)S(1)} %project.10), channel_id=1, source_target_pairs={{0,1},{1,0},{2,3},{3,2},{4,5},{5,4},{6,7},{7,6},{8,9},{9,8},{10,11... | collective-permute-start | bytes 688136 | tf_op jit(solution)/shard_map/ppermute | solution.py:360
  31.6 4.4 %collective-permute-start.4 = (bf16[128,896]{1,0:T(8,128)(2,1)S(1)}, bf16[128,896]{1,0:T(8,128)(2,1)S(1)}, u32[]{:S(2)}, u32[]{:S(2)}) collective-permute-start(bf16[128,896]{1,0:T(8,128)(2,1)S(1)} %get-tuple-element.30), channel_id=1, source_target_pairs={{0,1},{1,0},{2,3},{3,2},{4,5},{5,4},{6,7},{7,6},{8,9},{9,8},{10,11... | collective-permute-start | bytes 688136 | tf_op jit(solution)/shard_map/ppermute | solution.py:360
  31.6 4.3 %collective-permute-start.5 = (bf16[128,896]{1,0:T(8,128)(2,1)S(1)}, bf16[128,896]{1,0:T(8,128)(2,1)S(1)}, u32[]{:S(2)}, u32[]{:S(2)}) collective-permute-start(bf16[128,896]{1,0:T(8,128)(2,1)S(1)} %get-tuple-element.31), channel_id=1, source_target_pairs={{0,1},{1,0},{2,3},{3,2},{4,5},{5,4},{6,7},{7,6},{8,9},{9,8},{10,11... | collective-permute-start | bytes 688136 | tf_op jit(solution)/shard_map/ppermute | solution.py:360
  32.9 7.9 %collective-permute-start.9 = (bf16[64,896]{1,0:T(8,128)(2,1)S(1)}, bf16[64,896]{1,0:T(8,128)(2,1)S(1)}, u32[]{:S(2)}, u32[]{:S(2)}) collective-permute-start(bf16[64,896]{1,0:T(8,128)(2,1)S(1)} %get-tuple-element.38), channel_id=1, source_target_pairs={{0,2},{1,3},{2,0},{3,1},{4,6},{5,7},{6,4},{7,5},{8,10},{9,11},{10,... | collective-permute-start | bytes 344072 | tf_op jit(solution)/shard_map/ppermute | solution.py:360
  34.4 4.9 %collective-permute-start.11 = (bf16[64,896]{1,0:T(8,128)(2,1)S(1)}, bf16[64,896]{1,0:T(8,128)(2,1)S(1)}, u32[]{:S(2)}, u32[]{:S(2)}) collective-permute-start(bf16[64,896]{1,0:T(8,128)(2,1)S(1)} %get-tuple-element.41), channel_id=1, source_target_pairs={{0,4},{1,5},{2,6},{3,7},{4,0},{5,1},{6,2},{7,3},{8,12},{9,13},{10,... | collective-permute-start | bytes 344072 | tf_op jit(solution)/shard_map/ppermute | solution.py:360
  37.2 7.7 %collective-permute-start.7 = (bf16[64,896]{1,0:T(8,128)(2,1)S(1)}, bf16[64,896]{1,0:T(8,128)(2,1)S(1)}, u32[]{:S(2)}, u32[]{:S(2)}) collective-permute-start(bf16[64,896]{1,0:T(8,128)(2,1)S(1)} %get-tuple-element.36), channel_id=1, source_target_pairs={{0,2},{1,3},{2,0},{3,1},{4,6},{5,7},{6,4},{7,5},{8,10},{9,11},{10,... | collective-permute-start | bytes 344072 | tf_op jit(solution)/shard_map/ppermute | solution.py:360
  37.9 5.3 %collective-permute-start.13 = (bf16[64,896]{1,0:T(8,128)(2,1)S(1)}, bf16[64,896]{1,0:T(8,128)(2,1)S(1)}, u32[]{:S(2)}, u32[]{:S(2)}) collective-permute-start(bf16[64,896]{1,0:T(8,128)(2,1)S(1)} %get-tuple-element.42), channel_id=1, source_target_pairs={{0,4},{1,5},{2,6},{3,7},{4,0},{5,1},{6,2},{7,3},{8,12},{9,13},{10,... | collective-permute-start | bytes 344072 | tf_op jit(solution)/shard_map/ppermute | solution.py:360
  39.2 3.3 %collective-permute-start.6 = (bf16[128,896]{1,0:T(8,128)(2,1)S(1)}, bf16[128,896]{1,0:T(8,128)(2,1)S(1)}, u32[]{:S(2)}, u32[]{:S(2)}) collective-permute-start(bf16[128,896]{1,0:T(8,128)(2,1)S(1)} %project.8), channel_id=1, source_target_pairs={{0,1},{1,0},{2,3},{3,2},{4,5},{5,4},{6,7},{7,6},{8,9},{9,8},{10,11... | collective-permute-start | bytes 688136 | tf_op jit(solution)/shard_map/ppermute | solution.py:360
  39.3 5.6 %collective-permute-start.12 = (bf16[64,896]{1,0:T(8,128)(2,1)S(1)}, bf16[64,896]{1,0:T(8,128)(2,1)S(1)}, u32[]{:S(2)}, u32[]{:S(2)}) collective-permute-start(bf16[64,896]{1,0:T(8,128)(2,1)S(1)} %add_convert_fusion.1), channel_id=1, source_target_pairs={{0,2},{1,3},{2,0},{3,1},{4,6},{5,7},{6,4},{7,5},{8,10},{9,11},{10,... | collective-permute-start | bytes 344072 | tf_op jit(solution)/shard_map/ppermute | solution.py:360
  40.9 5.3 %collective-permute-start.10 = (bf16[64,896]{1,0:T(8,128)(2,1)S(1)}, bf16[64,896]{1,0:T(8,128)(2,1)S(1)}, u32[]{:S(2)}, u32[]{:S(2)}) collective-permute-start(bf16[64,896]{1,0:T(8,128)(2,1)S(1)} %add_convert_fusion.3), channel_id=1, source_target_pairs={{0,4},{1,5},{2,6},{3,7},{4,0},{5,1},{6,2},{7,3},{8,12},{9,13},{10,... | collective-permute-start | bytes 344072 | tf_op jit(solution)/shard_map/ppermute | solution.py:360
